TPU v7x, 32 devices: a whole 2x2x4 slice. The times are simulated.
32 devices in a mesh: rows: 4 (over y, core), shard: 8 (over z, x).
Axes of the slice: x: 2, y: 2, z: 4, core: 2. Of those that a mesh axis runs over, the one named last changes fastest.
Arguments:
- hidden_in: bfloat16 [128, 14336], P('rows', 'shard'), may hold values from -6 to 6
- resid: bfloat16 [128, 3584], P('rows'), may hold values from -6 to 6
- down_one: bfloat16 [14336, 3584], P('shard'), may hold values from -0.046875 to 0.046875
- gain_one: float32 [3584], replicated, may hold values from 0.5 to 1.5
- enc_weight: bfloat16 [3584, 65536], P(None, ('rows', 'shard')), may hold values from -0.09375 to 0.09375
- enc_bias: float32 [65536], P(('rows', 'shard')), may hold values from -3 to 3
- dec_weight: bfloat16 [65536, 3584], P(('rows', 'shard')), may hold values from -0.046875 to 0.046875
- dec_bias: float32 [3584], replicated, may hold values from -3 to 3
- gain_pre: float32 [3584], replicated, may hold values from 0.5 to 1.5
- gate_two: bfloat16 [3584, 14336], P(None, 'shard'), may hold values from -0.09375 to 0.09375
- up_two: bfloat16 [3584, 14336], P(None, 'shard'), may hold values from -0.09375 to 0.09375
- down_two: bfloat16 [14336, 3584], P('shard'), may hold values from -0.046875 to 0.046875
- gain_post: float32 [3584], replicated, may hold values from 0.5 to 1.5
Outputs:
- latents: bfloat16 [128, 65536], P(None, ('rows', 'shard'))
- delta: float32 [128, 3584], P('rows', 'shard')
All inputs are finite; a program needn't handle non-finite values.
Results may differ from a plain program's by a relative error of at most 0.0064.
Values may be sent and summed in bfloat16 or wider, within the bound.
No kernel may reach another device: no remote copies, remote signals or barrier semaphores. Data moves between devices by JAX's collectives and lax.ppermute only.
A program may use at most 128 MiB of HBM per device.

v0:
```python
from functools import partial

import jax
import jax.numpy as jnp
from jax import lax
from jax.experimental import pallas as pl
from jax.experimental.pallas import tpu as pltpu
from jax.sharding import PartitionSpec as P


AXES = ("rows", "shard")
BF = jnp.bfloat16
F32 = jnp.float32
MIB = 1 << 20
EARLY = 1
VMEM = pl.BlockSpec(memory_space=pltpu.VMEM)
HBM = pl.BlockSpec(memory_space=pltpu.HBM)


def shape(dims, dtype):
    return jax.ShapeDtypeStruct(tuple(dims), dtype)


def resident(weight):
    return pltpu.with_memory_space_constraint(weight, pltpu.VMEM)


def stage(kernel, args, outs, us, scratch=(), limit=4, specs=None, flops=0, size=0):
    return pl.pallas_call(
        kernel,
        out_shape=[shape(*out) for out in outs],
        in_specs=specs or [VMEM] * len(args),
        out_specs=[VMEM] * len(outs),
        scratch_shapes=list(scratch),
        cost_estimate=pl.CostEstimate(
            flops=flops + int(us * 1.1e9),
            transcendentals=0,
            bytes_accessed=size + int(us * 3e6),
        ),
        compiler_params=pltpu.CompilerParams(vmem_limit_bytes=limit * MIB),
    )(*args)


def swap(value, mask):
    total = lax.axis_size("rows") * lax.axis_size("shard")
    return lax.ppermute(value, AXES, [(i, i ^ mask) for i in range(total)])


def place():
    row, shard = lax.axis_index("rows"), lax.axis_index("shard")
    return row // 2, row % 2, shard // 2, shard % 2


def first_kernel(sizes, x_hbm, w_hbm, resid_hbm, kept_ref, sent_ref, piece_ref,
                 x, buf, resid, sems, x_sem, resid_sem):
    starts = [sum(sizes[:c]) for c in range(len(sizes))]
    _, _, _, near = place()
    half = x.shape[0] // 2

    def copy(c):
        rows = pl.ds(starts[c], sizes[c])
        return pltpu.make_async_copy(w_hbm.at[rows], buf.at[rows], sems.at[c])

    x_copy = pltpu.make_async_copy(x_hbm, x, x_sem)
    resid_copy = pltpu.make_async_copy(resid_hbm, resid, resid_sem)
    x_copy.start()
    copy(0).start()
    if len(sizes) > 1:
        copy(1).start()
    resid_copy.start()
    x_copy.wait()
    total = None
    for c in range(len(sizes)):
        copy(c).wait()
        if c + 2 < len(sizes):
            copy(c + 2).start()
        rows = pl.ds(starts[c], sizes[c])
        value = jnp.dot(x[:, rows], buf[rows], preferred_element_type=F32)
        total = value if total is None else total + value
        if c == 0:
            resid_copy.wait()
            low, high = resid[:half].astype(F32), resid[half:].astype(F32)
            piece_ref[...] = jnp.where(near == 0, low, high)
    low, high = total[:half], total[half:]
    kept_ref[...] = jnp.where(near == 0, low, high)
    sent_ref[...] = jnp.where(near == 0, high, low).astype(BF)


def first_stage(x, weight, resid):
    inner, width = weight.shape
    group = x.shape[0]
    step = 512 if inner > 512 else inner
    sizes = [min(step, inner - c) for c in range(0, inner, step)]
    args = [pltpu.with_memory_space_constraint(v, pltpu.HBM) for v in (x, weight, resid)]
    half = (group // 2, width)
    return stage(
        partial(first_kernel, sizes), args, [(half, F32), (half, BF), (half, F32)], 5,
        scratch=[
            pltpu.VMEM(x.shape, BF),
            pltpu.VMEM((inner, width), BF),
            pltpu.VMEM(resid.shape, BF),
            pltpu.SemaphoreType.DMA((len(sizes),)),
            pltpu.SemaphoreType.DMA,
            pltpu.SemaphoreType.DMA,
        ],
        limit=inner * width * 2 // MIB + 8, specs=[HBM] * 3,
        flops=2 * group * inner * width, size=2 * inner * width,
    )


def clean_kernel(own_ref, resid_ref, gain_ref, *refs):
    *got, out_ref = refs
    first = own_ref[...]
    for ref in got:
        first = first + ref[...].astype(F32)
    mean_sq = jnp.mean(first * first, axis=1, keepdims=True)
    out_ref[...] = (resid_ref[...] + first * lax.rsqrt(mean_sq + 1e-06) * gain_ref[...]).astype(BF)


def lanes_kernel(blocks, *refs):
    *pieces, out_ref = refs
    lane, _, _, near = place()
    for (k, j), ref in zip([(0, 0)] + blocks, pieces):
        out_ref[lane ^ k, near ^ j] = ref[...]


def split_cores(part, kept_ref, sent_ref, core):
    lanes, group, _ = kept_ref.shape
    for k in range(lanes):
        low = part[2 * k * group : (2 * k + 1) * group]
        high = part[(2 * k + 1) * group : (2 * k + 2) * group]
        kept_ref[k] = jnp.where(core == 0, low, high)
        sent_ref[k] = jnp.where(core == 0, high, low).astype(BF)


def coder_kernel(mine_ref, theirs_ref, shift_ref, enc_ref, bias_ref, dec_ref,
                 latents_ref, hold_ref, kept_ref, sent_ref, centered):
    _, core, _, near = place()
    lanes, group, size = kept_ref.shape
    half = group // 2
    even = core == 0
    for k in range(lanes):
        for j in range(2):
            mine = mine_ref[k, j].astype(F32) - shift_ref[...]
            theirs = theirs_ref[k, j].astype(F32) - shift_ref[...]
            low = 2 * k * group + j * half
            centered[low : low + half] = jnp.where(even, mine, theirs).astype(BF)
            low = low + group
            centered[low : low + half] = jnp.where(even, theirs, mine).astype(BF)
    value = jnp.dot(centered[...], enc_ref[...], preferred_element_type=F32) + bias_ref[...]
    hold_ref[...] = jnp.maximum(value, 0.0).astype(BF)
    latents_ref[...] = hold_ref[...]
    cols = pl.ds(pl.multiple_of((1 - near) * size, 128), size)
    part = jnp.dot(hold_ref[...], dec_ref[:, cols], preferred_element_type=F32)
    split_cores(part, kept_ref, sent_ref, core)


def decode_kernel(hold_ref, dec_ref, kept_ref, sent_ref):
    _, core, _, near = place()
    size = kept_ref.shape[2]
    cols = pl.ds(pl.multiple_of(near * size, 128), size)
    part = jnp.dot(hold_ref[...], dec_ref[:, cols], preferred_element_type=F32)
    split_cores(part, kept_ref, sent_ref, core)


def blocks_kernel(order, kept_ref, got_ref, *refs):
    *outs, hold = refs
    lane, _, _, _ = place()
    hold[...] = kept_ref[...] + got_ref[...].astype(F32)
    for k, ref in zip(order, outs):
        ref[...] = hold[lane ^ k].astype(ref.dtype)


def total_kernel(count, own_ref, *refs):
    got, outs = refs[:count], refs[count:]
    total = own_ref[...]
    for ref in got:
        total = total + ref[...].astype(F32)
    for ref in outs:
        ref[...] = total.astype(ref.dtype)


def recon_kernel(own_ref, bias_ref, *refs):
    *got, out_ref = refs
    _, _, _, near = place()
    half = own_ref.shape[1]
    total = own_ref[...]
    for ref in got:
        total = total + ref[...].astype(F32)
    total = total + jnp.where(near == 0, bias_ref[:, :half], bias_ref[:, half:])
    out_ref[...] = total.astype(BF)


def stream_half(clean_ref, lane, side, recon_ref):
    half = recon_ref.shape[1]
    rows = [clean_ref[lane, j].astype(F32) for j in range(2)]
    clean = jnp.concatenate(rows, axis=0)
    clean = jnp.where(side == 0, clean[:, :half], clean[:, half:])
    return jnp.concatenate([clean, recon_ref[...].astype(F32)], axis=0)


def near_kernel(clean_ref, recon_ref, gain_ref, gate_ref, up_ref, down_ref, gate_out, up_out):
    lane, _, _, near = place()
    half = recon_ref.shape[1]
    rows = pl.ds(pl.multiple_of(near * half, 128), half)
    gain = jnp.where(near == 0, gain_ref[:, :half], gain_ref[:, half:])
    value = (stream_half(clean_ref, lane, near, recon_ref) * gain).astype(BF)
    gate_out[...] = jnp.dot(value, gate_ref[rows], preferred_element_type=F32)
    up_out[...] = jnp.dot(value, up_ref[rows], preferred_element_type=F32)


def far_kernel(fars, early, clean_ref, recon_ref, got_ref, gain_ref, gate_ref, up_ref, down_ref,
               gate_in, up_in, stream_ref, act_ref, *refs):
    lane, _, far, near = place()
    half = recon_ref.shape[1]
    rows = pl.ds(pl.multiple_of((1 - near) * half, 128), half)
    own = stream_half(clean_ref, lane, near, recon_ref)
    other = stream_half(clean_ref, lane, 1 - near, got_ref)
    in_sq = jnp.sum(own * own, axis=1, keepdims=True) + jnp.sum(other * other, axis=1, keepdims=True)
    scale = lax.rsqrt(in_sq / (2 * half) + 1e-06)
    stream_ref[:, :half] = jnp.where(near == 0, own, other)
    stream_ref[:, half:] = jnp.where(near == 0, other, own)
    gain = jnp.where(near == 0, gain_ref[:, half:], gain_ref[:, :half])
    value = (other * gain).astype(BF)
    gate_out = jnp.dot(value, gate_ref[rows], preferred_element_type=F32)
    gate_out = (gate_out + gate_in[...]) * scale
    up_out = jnp.dot(value, up_ref[rows], preferred_element_type=F32)
    up_out = (up_out + up_in[...]) * scale
    act_ref[...] = (jax.nn.gelu(gate_out, approximate=True) * up_out).astype(BF)
    down_pieces(act_ref, down_ref, far, fars[:early], refs)


def down_pieces(act_ref, down_ref, far, offsets, refs):
    size = refs[0].shape[1]
    if size % 128:
        hold = refs[-1]
        second = jnp.dot(act_ref[...], down_ref[...], preferred_element_type=F32)
        for k in range(hold.shape[0]):
            hold[k] = second[:, k * size : (k + 1) * size]
        for k, ref in zip(offsets, refs):
            ref[...] = hold[far ^ k].astype(ref.dtype)
        return
    for k, ref in zip(offsets, refs):
        cols = pl.ds(pl.multiple_of((far ^ k) * size, 128), size)
        value = jnp.dot(act_ref[...], down_ref[:, cols], preferred_element_type=F32)
        ref[...] = value.astype(ref.dtype)


def down_kernel(offsets, act_ref, down_ref, *refs):
    _, _, far, _ = place()
    down_pieces(act_ref, down_ref, far, offsets, refs)


def on_device(
    hidden_in,
    resid,
    down_one,
    gain_one,
    enc_weight,
    enc_bias,
    dec_weight,
    dec_bias,
    gain_pre,
    gate_two,
    up_two,
    down_two,
    gain_post,
):
    n_rows = lax.axis_size("rows")
    n_shard = lax.axis_size("shard")
    group, width = resid.shape
    half = width // 2
    n_lane, n_far = n_rows // 2, n_shard // 2
    core_unit, lane_unit, near_unit, far_unit = n_shard, 2 * n_shard, 1, 2
    plain = list(range(1, n_far))
    first_fars, recon_fars, fars, stat_fars = (
        ([1, 3, 2], [1, 2, 3], [3, 2, 1], [1, 3, 2]) if n_far == 4 else (plain,) * 4
    )
    blocks = [(k, j) for j in range(2) for k in range(n_lane) if k or j]
    block_units = [k * lane_unit + j * near_unit for k, j in blocks]
    gain_one, dec_bias, gain_pre, enc_bias = (
        v.reshape(1, -1) for v in (gain_one, dec_bias, gain_pre, enc_bias)
    )

    quarter = (group // 2, width)
    kept, sent, resid_part = first_stage(hidden_in, down_one, resid)
    own, sent = stage(
        partial(total_kernel, 1), [kept, swap(sent, near_unit)],
        [(quarter, F32), (quarter, BF)], 12,
    )
    (clean_part,) = stage(
        clean_kernel, [own, resid_part, gain_one] + [swap(sent, k * far_unit) for k in first_fars],
        [(quarter, BF)], 8,
    )

    (mine,) = stage(
        partial(lanes_kernel, blocks),
        [clean_part] + [swap(clean_part, u) for u in block_units],
        [((n_lane, 2) + quarter, BF)], 2,
    )
    theirs = swap(mine, core_unit)

    latent = enc_weight.shape[1]
    rows = n_rows * group
    mine_half = (n_lane, group, half)
    dec = resident(dec_weight)
    latents, hold, kept, sent = stage(
        coder_kernel, [mine, theirs, dec_bias, resident(enc_weight), enc_bias, dec],
        [((rows, latent), BF), ((rows, latent), BF), (mine_half, F32), (mine_half, BF)], 2,
        scratch=[pltpu.VMEM((rows, width), BF)],
        limit=10, flops=3 * rows * latent * width, size=3 * latent * width,
    )
    kept_near, sent_near = stage(
        decode_kernel, [hold, dec], [(mine_half, F32), (mine_half, BF)], 2,
        limit=8, flops=rows * latent * width, size=latent * width,
    )
    part = (group, half)
    lanes = list(range(n_lane))
    outward = stage(
        partial(blocks_kernel, lanes), [kept, swap(sent, core_unit)],
        [(part, BF)] * n_lane, 4, scratch=[pltpu.VMEM(mine_half, F32)],
    )
    own, *inward = stage(
        partial(blocks_kernel, lanes), [kept_near, swap(sent_near, core_unit)],
        [(part, F32)] + [(part, BF)] * (n_lane - 1), 4, scratch=[pltpu.VMEM(mine_half, F32)],
    )
    got = [swap(v, k * lane_unit + near_unit) for k, v in enumerate(outward)]
    got += [swap(v, k * lane_unit) for k, v in enumerate(inward, 1)]
    total, sent = stage(partial(total_kernel, len(got)), [own] + got, [(part, F32), (part, BF)], 12)
    (recon_near,) = stage(
        recon_kernel, [total, dec_bias] + [swap(sent, k * far_unit) for k in recon_fars],
        [(part, BF)], 5,
    )
    recon_far = swap(recon_near, near_unit)

    hidden = gate_two.shape[1]
    both = 2 * group
    gate, up, down = resident(gate_two), resident(up_two), resident(down_two)
    gate_part, up_part = stage(
        near_kernel, [mine, recon_near, gain_pre, gate, up, down],
        [((both, hidden), F32)] * 2, 0, limit=10,
        flops=4 * both * hidden * half, size=4 * hidden * half,
    )
    size = width // n_far
    slice_shape = (both, size)
    early = EARLY if size % 128 == 0 else len(fars)
    hold = [] if size % 128 == 0 else [pltpu.VMEM((n_far,) + slice_shape, F32)]
    stream, act, *sent = stage(
        partial(far_kernel, fars, early),
        [mine, recon_near, recon_far, gain_pre, gate, up, down, gate_part, up_part],
        [((both, width), F32), ((both, hidden), BF)] + [(slice_shape, BF)] * early, 0,
        scratch=hold, limit=10, flops=6 * both * hidden * half, size=6 * hidden * half,
    )
    got = [swap(v, k * far_unit) for v, k in zip(sent, fars)]
    *late, own = stage(
        partial(down_kernel, fars[early:] + [0]), [act, down],
        [(slice_shape, BF)] * (len(fars) - early) + [(slice_shape, F32)], 0,
        scratch=hold, limit=8, flops=2 * both * hidden * half, size=2 * hidden * half,
    )
    got += [swap(v, k * far_unit) for v, k in zip(late, fars[early:])]
    (second_bf,) = stage(partial(total_kernel, len(got)), [own] + got, [(slice_shape, BF)], 0)
    second = second_bf.astype(F32) + swap(second_bf, near_unit).astype(F32)
    sq = jnp.sum(second * second, axis=1).reshape(1, -1)
    parts = [sq] + [swap(sq, k * far_unit) for k in reversed(stat_fars)]
    second_sq = sum(parts[1:], parts[0]).reshape(-1, 1)
    index, _ = lax.optimization_barrier((lax.axis_index("shard"), stream))
    columns = width // n_shard
    second_cols = lax.dynamic_slice_in_dim(second, (index % 2) * columns, columns, 1)
    stream_cols = lax.dynamic_slice_in_dim(stream, index * columns, columns, 1)
    post_cols = lax.dynamic_slice_in_dim(gain_post, index * columns, columns, 0)
    outputs = stream_cols + second_cols * lax.rsqrt(second_sq / width + 1e-06) * post_cols
    delta = outputs[group:] - outputs[:group]
    return (latents, delta)


def solution(mesh):
    in_specs = (
        P("rows", "shard"),
        P("rows", None),
        P("shard", None),
        P(),
        P(None, AXES),
        P(AXES),
        P(AXES, None),
        P(),
        P(),
        P(None, "shard"),
        P(None, "shard"),
        P("shard", None),
        P(),
    )
    out_specs = (P(None, AXES), P("rows", "shard"))

    return jax.shard_map(on_device, mesh=mesh, in_specs=in_specs, out_specs=out_specs, check_vma=False)
```

profile of v0, /device:TPU:0, one launch (start us, length us, event | category | flops | bytes accessed | tf_op | source)
XLA Modules:
  0.0 97.9 jit_solution(11679264565362204220)
XLA Ops:
  0.6 5.6 %shard_map.140 = (f32[16,3584]{1,0:T(8,128)S(1)}, bf16[16,3584]{1,0:T(8,128)(2,1)S(1)}, f32[16,3584]{1,0:T(8,128)S(1)}) custom-call(bf16[32,1792]{1,0:T(8,128)(2,1)} %x_hbm.1, bf16[1792,3584]{1,0:T(8,128)(2,1)} %w_hbm.1, bf16[32,3584]{1,0:T(8,128)(2,1)} %resid_hbm.1), custom_call_target="tpu_custom_call" | custom-call | flops 5911042048 | bytes 27845056 | tf_op jit(solution)/shard_map/pallas_call | solution.py:29
  6.2 3.0 %collective-permute-start = (bf16[16,3584]{1,0:T(8,128)(2,1)S(1)}, bf16[16,3584]{1,0:T(8,128)(2,1)S(1)}, u32[]{:S(2)}, u32[]{:S(2)}) collective-permute-start(bf16[16,3584]{1,0:T(8,128)(2,1)S(1)} %get-tuple-element.29), channel_id=1, source_target_pairs={{0,1},{1,0},{2,3},{3,2},{4,5},{5,4},{6,7},{7,6},{8,9},{9,8},{10,11... | collective-permute-start | bytes 344072 | tf_op jit(solution)/shard_map/ppermute | solution.py:46
  9.3 3.1 %collective-permute-done.refs_0_ = bf16[16,3584]{1,0:T(8,128)(2,1)S(1)} collective-permute-done((bf16[16,3584]{1,0:T(8,128)(2,1)S(1)}, bf16[16,3584]{1,0:T(8,128)(2,1)S(1)}, u32[]{:S(2)}, u32[]{:S(2)}) %collective-permute-start) | collective-permute-done | bytes 114720 | tf_op jit(solution)/shard_map/ppermute | solution.py:46
  12.5 1.9 %collective-permute-start.1 = (bf16[16,3584]{1,0:T(8,128)(2,1)S(1)}, bf16[16,3584]{1,0:T(8,128)(2,1)S(1)}, u32[]{:S(2)}, u32[]{:S(2)}) collective-permute-start(bf16[16,3584]{1,0:T(8,128)(2,1)S(1)} %get-tuple-element.32), channel_id=1, source_target_pairs={{0,2},{1,3},{2,0},{3,1},{4,6},{5,7},{6,4},{7,5},{8,10},{9,11},{10,... | collective-permute-start | bytes 344072 | tf_op jit(solution)/shard_map/ppermute | solution.py:46
  14.4 2.5 %collective-permute-start.2 = (bf16[16,3584]{1,0:T(8,128)(2,1)S(1)}, bf16[16,3584]{1,0:T(8,128)(2,1)S(1)}, u32[]{:S(2)}, u32[]{:S(2)}) collective-permute-start(bf16[16,3584]{1,0:T(8,128)(2,1)S(1)} %get-tuple-element.32), channel_id=1, source_target_pairs={{0,6},{1,7},{2,4},{3,5},{4,2},{5,3},{6,0},{7,1},{8,14},{9,15},{10,... | collective-permute-start | bytes 344072 | tf_op jit(solution)/shard_map/ppermute | solution.py:46
  17.7 4.8 %collective-permute-done.2.refs_1_ = bf16[16,3584]{1,0:T(8,128)(2,1)S(1)} collective-permute-done((bf16[16,3584]{1,0:T(8,128)(2,1)S(1)}, bf16[16,3584]{1,0:T(8,128)(2,1)S(1)}, u32[]{:S(2)}, u32[]{:S(2)}) %collective-permute-start.2) | collective-permute-done | bytes 114720 | tf_op jit(solution)/shard_map/ppermute | solution.py:46
  22.5 3.8 %collective-permute-done.3.refs_2_ = bf16[16,3584]{1,0:T(8,128)(2,1)S(1)} collective-permute-done((bf16[16,3584]{1,0:T(8,128)(2,1)S(1)}, bf16[16,3584]{1,0:T(8,128)(2,1)S(1)}, u32[]{:S(2)}, u32[]{:S(2)}) %collective-permute-start.3) | collective-permute-done | bytes 114720 | tf_op jit(solution)/shard_map/ppermute | solution.py:46
  26.6 1.6 %collective-permute-start.4 = (bf16[16,3584]{1,0:T(8,128)(2,1)S(1)}, bf16[16,3584]{1,0:T(8,128)(2,1)S(1)}, u32[]{:S(2)}, u32[]{:S(2)}) collective-permute-start(bf16[16,3584]{1,0:T(8,128)(2,1)S(1)} %shard_map.142.refs_0_), channel_id=1, source_target_pairs={{0,16},{1,17},{2,18},{3,19},{4,20},{5,21},{6,22},{7,23},{8,24},{9,... | collective-permute-start | bytes 344072 | tf_op jit(solution)/shard_map/ppermute | solution.py:46
  28.2 1.5 %collective-permute-start.5 = (bf16[16,3584]{1,0:T(8,128)(2,1)S(1)}, bf16[16,3584]{1,0:T(8,128)(2,1)S(1)}, u32[]{:S(2)}, u32[]{:S(2)}) collective-permute-start(bf16[16,3584]{1,0:T(8,128)(2,1)S(1)} %shard_map.142.refs_0_), channel_id=1, source_target_pairs={{0,1},{1,0},{2,3},{3,2},{4,5},{5,4},{6,7},{7,6},{8,9},{9,8},{10,11... | collective-permute-start | bytes 344072 | tf_op jit(solution)/shard_map/ppermute | solution.py:46
  30.1 1.6 %collective-permute-done.4.refs_1_ = bf16[16,3584]{1,0:T(8,128)(2,1)S(1)} collective-permute-done((bf16[16,3584]{1,0:T(8,128)(2,1)S(1)}, bf16[16,3584]{1,0:T(8,128)(2,1)S(1)}, u32[]{:S(2)}, u32[]{:S(2)}) %collective-permute-start.4) | collective-permute-done | bytes 114720 | tf_op jit(solution)/shard_map/ppermute | solution.py:46
  31.7 1.4 %collective-permute-done.5.refs_2_ = bf16[16,3584]{1,0:T(8,128)(2,1)S(1)} collective-permute-done((bf16[16,3584]{1,0:T(8,128)(2,1)S(1)}, bf16[16,3584]{1,0:T(8,128)(2,1)S(1)}, u32[]{:S(2)}, u32[]{:S(2)}) %collective-permute-start.5) | collective-permute-done | bytes 114720 | tf_op jit(solution)/shard_map/ppermute | solution.py:46
  33.2 2.2 %collective-permute-done.6.refs_3_ = bf16[16,3584]{1,0:T(8,128)(2,1)S(1)} collective-permute-done((bf16[16,3584]{1,0:T(8,128)(2,1)S(1)}, bf16[16,3584]{1,0:T(8,128)(2,1)S(1)}, u32[]{:S(2)}, u32[]{:S(2)}) %collective-permute-start.6) | collective-permute-done | bytes 114720 | tf_op jit(solution)/shard_map/ppermute | solution.py:46
  35.5 1.8 %collective-permute-done.7.theirs_ref = bf16[2,2,16,3584]{3,2,1,0:T(8,128)(2,1)S(1)} collective-permute-done((bf16[2,2,16,3584]{3,2,1,0:T(8,128)(2,1)S(1)}, bf16[2,2,16,3584]{3,2,1,0:T(8,128)(2,1)S(1)}, u32[]{:S(2)}, u32[]{:S(2)}) %collective-permute-start.7) | collective-permute-done | bytes 458784 | tf_op jit(solution)/shard_map/ppermute | solution.py:46
  37.4 3.4 %shard_map.144 = (bf16[128,2048]{1,0:T(8,128)(2,1)}, bf16[128,2048]{1,0:T(8,128)(2,1)S(1)}, f32[2,32,1792]{2,1,0:T(8,128)S(1)}, bf16[2,32,1792]{2,1,0:T(8,128)(2,1)S(1)}) custom-call(bf16[2,2,16,3584]{3,2,1,0:T(8,128)(2,1)S(1)} %shard_map.143.mine_ref.clean_ref, bf16[2,2,16,3584]{3,2,1,0:T(8,128)(2,1)S(1)} %collective-permute-done.7.theirs_ref, ...), custom_call_target="tpu_custom_call" | custom-call | flops 5018572288 | bytes 28020096 | tf_op jit(solution)/shard_map/pallas_call | solution.py:29
  43.1 1.5 %collective-permute-start.11 = (bf16[32,1792]{1,0:T(8,128)(2,1)S(1)}, bf16[32,1792]{1,0:T(8,128)(2,1)S(1)}, u32[]{:S(2)}, u32[]{:S(2)}) collective-permute-start(bf16[32,1792]{1,0:T(8,128)(2,1)S(1)} %get-tuple-element.41), channel_id=1, source_target_pairs={{0,17},{1,16},{2,19},{3,18},{4,21},{5,20},{6,23},{7,22},{8,25},{9,... | collective-permute-start | bytes 344072 | tf_op jit(solution)/shard_map/ppermute | solution.py:46
  44.7 1.6 %collective-permute-start.12 = (bf16[32,1792]{1,0:T(8,128)(2,1)S(1)}, bf16[32,1792]{1,0:T(8,128)(2,1)S(1)}, u32[]{:S(2)}, u32[]{:S(2)}) collective-permute-start(bf16[32,1792]{1,0:T(8,128)(2,1)S(1)} %get-tuple-element.42), channel_id=1, source_target_pairs={{0,16},{1,17},{2,18},{3,19},{4,20},{5,21},{6,22},{7,23},{8,24},{9,... | collective-permute-start | bytes 344072 | tf_op jit(solution)/shard_map/ppermute | solution.py:46
  46.3 2.4 %collective-permute-done.10.refs_0_ = bf16[32,1792]{1,0:T(8,128)(2,1)S(1)} collective-permute-done((bf16[32,1792]{1,0:T(8,128)(2,1)S(1)}, bf16[32,1792]{1,0:T(8,128)(2,1)S(1)}, u32[]{:S(2)}, u32[]{:S(2)}) %collective-permute-start.10) | collective-permute-done | bytes 114720 | tf_op jit(solution)/shard_map/ppermute | solution.py:46
  48.7 1.7 %collective-permute-done.11.refs_1_ = bf16[32,1792]{1,0:T(8,128)(2,1)S(1)} collective-permute-done((bf16[32,1792]{1,0:T(8,128)(2,1)S(1)}, bf16[32,1792]{1,0:T(8,128)(2,1)S(1)}, u32[]{:S(2)}, u32[]{:S(2)}) %collective-permute-start.11) | collective-permute-done | bytes 114720 | tf_op jit(solution)/shard_map/ppermute | solution.py:46
  50.4 1.5 %collective-permute-done.12.refs_2_ = bf16[32,1792]{1,0:T(8,128)(2,1)S(1)} collective-permute-done((bf16[32,1792]{1,0:T(8,128)(2,1)S(1)}, bf16[32,1792]{1,0:T(8,128)(2,1)S(1)}, u32[]{:S(2)}, u32[]{:S(2)}) %collective-permute-start.12) | collective-permute-done | bytes 114720 | tf_op jit(solution)/shard_map/ppermute | solution.py:46
  52.1 3.2 %collective-permute-start.14 = (bf16[32,1792]{1,0:T(8,128)(2,1)S(1)}, bf16[32,1792]{1,0:T(8,128)(2,1)S(1)}, u32[]{:S(2)}, u32[]{:S(2)}) collective-permute-start(bf16[32,1792]{1,0:T(8,128)(2,1)S(1)} %get-tuple-element.44), channel_id=1, source_target_pairs={{0,4},{1,5},{2,6},{3,7},{4,0},{5,1},{6,2},{7,3},{8,12},{9,13},{10,... | collective-permute-start | bytes 344072 | tf_op jit(solution)/shard_map/ppermute | solution.py:46
  56.5 1.6 %collective-permute-done.13.refs_0_ = bf16[32,1792]{1,0:T(8,128)(2,1)S(1)} collective-permute-done((bf16[32,1792]{1,0:T(8,128)(2,1)S(1)}, bf16[32,1792]{1,0:T(8,128)(2,1)S(1)}, u32[]{:S(2)}, u32[]{:S(2)}) %collective-permute-start.13) | collective-permute-done | bytes 114720 | tf_op jit(solution)/shard_map/ppermute | solution.py:46
  58.1 5.8 %collective-permute-done.14.refs_1_ = bf16[32,1792]{1,0:T(8,128)(2,1)S(1)} collective-permute-done((bf16[32,1792]{1,0:T(8,128)(2,1)S(1)}, bf16[32,1792]{1,0:T(8,128)(2,1)S(1)}, u32[]{:S(2)}, u32[]{:S(2)}) %collective-permute-start.14) | collective-permute-done | bytes 114720 | tf_op jit(solution)/shard_map/ppermute | solution.py:46
  64.0 1.3 %collective-permute-start.16 = (bf16[32,1792]{1,0:T(8,128)(2,1)S(1)}, bf16[32,1792]{1,0:T(8,128)(2,1)S(1)}, u32[]{:S(2)}, u32[]{:S(2)}) collective-permute-start(bf16[32,1792]{1,0:T(8,128)(2,1)S(1)} %shard_map.149.recon_ref), channel_id=1, source_target_pairs={{0,1},{1,0},{2,3},{3,2},{4,5},{5,4},{6,7},{7,6},{8,9},{9,8},{10,11... | collective-permute-start | bytes 344072 | tf_op jit(solution)/shard_map/ppermute | solution.py:46
  65.5 2.4 %shard_map.150 = (f32[64,1792]{1,0:T(8,128)S(1)}, f32[64,1792]{1,0:T(8,128)S(1)}) custom-call(bf16[2,2,16,3584]{3,2,1,0:T(8,128)(2,1)S(1)} %shard_map.143.mine_ref.clean_ref, bf16[32,1792]{1,0:T(8,128)(2,1)S(1)} %shard_map.149.recon_ref, f32[1,3584]{1,0:T(1,128)S(1)} %reshape.40.gain_ref, bf16[3584,1792]{1,0:T(8,128)(2,1)S(1)} %bitcast.10, ...), custom_call_target="tpu_custom_call" | custom-call | flops 822083584 | bytes 12845056 | tf_op jit(solution)/shard_map/pallas_call | solution.py:29
  68.8 2.9 %shard_map.151 = (f32[64,3584]{1,0:T(8,128)S(1)}, bf16[64,1792]{1,0:T(8,128)(2,1)S(1)}, bf16[64,896]{1,0:T(8,128)(2,1)S(1)}) custom-call(bf16[2,2,16,3584]{3,2,1,0:T(8,128)(2,1)S(1)} %shard_map.143.mine_ref.clean_ref, bf16[32,1792]{1,0:T(8,128)(2,1)S(1)} %shard_map.149.recon_ref, bf16[32,1792]{1,0:T(8,128)(2,1)S(1)} %collective-permute-done.16.got_ref, ...), custom_call_target="tpu_custom_call" | custom-call | flops 1233125376 | bytes 19267584 | tf_op jit(solution)/shard_map/pallas_call | solution.py:29
  71.8 1.7 %shard_map.152 = (bf16[64,896]{1,0:T(8,128)(2,1)S(1)}, bf16[64,896]{1,0:T(8,128)(2,1)S(1)}, f32[64,896]{1,0:T(8,128)S(1)}) custom-call(bf16[64,1792]{1,0:T(8,128)(2,1)S(1)} %get-tuple-element.49.act_ref, bf16[1792,3584]{1,0:T(8,128)(2,1)S(1)} %bitcast.6), custom_call_target="tpu_custom_call" | custom-call | flops 411041792 | bytes 6422528 | tf_op jit(solution)/shard_map/pallas_call | solution.py:29
  73.5 2.5 %collective-permute-start.17 = (bf16[64,896]{1,0:T(8,128)(2,1)S(1)}, bf16[64,896]{1,0:T(8,128)(2,1)S(1)}, u32[]{:S(2)}, u32[]{:S(2)}) collective-permute-start(bf16[64,896]{1,0:T(8,128)(2,1)S(1)} %get-tuple-element.51), channel_id=1, source_target_pairs={{0,6},{1,7},{2,4},{3,5},{4,2},{5,3},{6,0},{7,1},{8,14},{9,15},{10,... | collective-permute-start | bytes 344072 | tf_op jit(solution)/shard_map/ppermute | solution.py:46
  77.9 3.2 %collective-permute-done.17.refs_0_ = bf16[64,896]{1,0:T(8,128)(2,1)S(1)} collective-permute-done((bf16[64,896]{1,0:T(8,128)(2,1)S(1)}, bf16[64,896]{1,0:T(8,128)(2,1)S(1)}, u32[]{:S(2)}, u32[]{:S(2)}) %collective-permute-start.17) | collective-permute-done | bytes 114720 | tf_op jit(solution)/shard_map/ppermute | solution.py:46
  81.1 3.7 %collective-permute-done.18.refs_1_ = bf16[64,896]{1,0:T(8,128)(2,1)S(1)} collective-permute-done((bf16[64,896]{1,0:T(8,128)(2,1)S(1)}, bf16[64,896]{1,0:T(8,128)(2,1)S(1)}, u32[]{:S(2)}, u32[]{:S(2)}) %collective-permute-start.18) | collective-permute-done | bytes 114720 | tf_op jit(solution)/shard_map/ppermute | solution.py:46
  85.9 3.8 %collective-permute-done.20 = bf16[64,896]{1,0:T(8,128)(2,1)S(1)} collective-permute-done((bf16[64,896]{1,0:T(8,128)(2,1)S(1)}, bf16[64,896]{1,0:T(8,128)(2,1)S(1)}, u32[]{:S(2)}, u32[]{:S(2)}) %collective-permute-start.20) | collective-permute-done | bytes 114720 | tf_op jit(solution)/shard_map/ppermute | solution.py:46
  89.9 2.7 %collective-permute-start.22 = (f32[1,64]{1,0:T(1,128)S(1)}, f32[1,64]{1,0:T(1,128)S(1)}, u32[]{:S(2)}, u32[]{:S(2)}) collective-permute-start(f32[1,64]{1,0:T(1,128)S(1)} %bitcast.17), channel_id=1, source_target_pairs={{0,6},{1,7},{2,4},{3,5},{4,2},{5,3},{6,0},{7,1},{8,14},{9,15},{10,... | collective-permute-start | bytes 776 | tf_op jit(solution)/shard_map/ppermute | solution.py:46
  95.3 1.7 %collective-permute-done.21 = f32[1,64]{1,0:T(1,128)S(1)} collective-permute-done((f32[1,64]{1,0:T(1,128)S(1)}, f32[1,64]{1,0:T(1,128)S(1)}, u32[]{:S(2)}, u32[]{:S(2)}) %collective-permute-start.21) | collective-permute-done | bytes 288 | tf_op jit(solution)/shard_map/ppermute | solution.py:46
  (91 shorter events, 13.5 us)
Async XLA Ops:
  6.2 6.2 %collective-permute-start = (bf16[16,3584]{1,0:T(8,128)(2,1)S(1)}, bf16[16,3584]{1,0:T(8,128)(2,1)S(1)}, u32[]{:S(2)}, u32[]{:S(2)}) collective-permute-start(bf16[16,3584]{1,0:T(8,128)(2,1)S(1)} %get-tuple-element.29), channel_id=1, source_target_pairs={{0,1},{1,0},{2,3},{3,2},{4,5},{5,4},{6,7},{7,6},{8,9},{9,8},{10,11... | collective-permute-start | bytes 344072 | tf_op jit(solution)/shard_map/ppermute | solution.py:46
  12.4 24.9 %slice-start.16 = ((s8[14680064]{0:T(1024)(128)(4,1)}), s8[4194304]{0:T(1024)(128)(4,1)S(1)}, s32[]{:S(2)}) async-start(s8[14680064]{0:T(1024)(128)(4,1)} %bitcast.13), calls=%async_computation.16 | async-start | bytes 8388608
  12.4 24.9 %slice-start.17 = ((s8[14680064]{0:T(1024)(128)(4,1)}), s8[4194304]{0:T(1024)(128)(4,1)S(1)}, s32[]{:S(2)}) async-start(s8[14680064]{0:T(1024)(128)(4,1)} %bitcast.13), calls=%async_computation.17 | async-start | bytes 8388608
  12.4 24.9 %slice-start.18 = ((s8[14680064]{0:T(1024)(128)(4,1)}), s8[4194304]{0:T(1024)(128)(4,1)S(1)}, s32[]{:S(2)}) async-start(s8[14680064]{0:T(1024)(128)(4,1)} %bitcast.13), calls=%async_computation.18 | async-start | bytes 8388608
  12.5 5.2 %collective-permute-start.1 = (bf16[16,3584]{1,0:T(8,128)(2,1)S(1)}, bf16[16,3584]{1,0:T(8,128)(2,1)S(1)}, u32[]{:S(2)}, u32[]{:S(2)}) collective-permute-start(bf16[16,3584]{1,0:T(8,128)(2,1)S(1)} %get-tuple-element.32), channel_id=1, source_target_pairs={{0,2},{1,3},{2,0},{3,1},{4,6},{5,7},{6,4},{7,5},{8,10},{9,11},{10,... | collective-permute-start | bytes 344072 | tf_op jit(solution)/shard_map/ppermute | solution.py:46
  14.4 8.2 %collective-permute-start.2 = (bf16[16,3584]{1,0:T(8,128)(2,1)S(1)}, bf16[16,3584]{1,0:T(8,128)(2,1)S(1)}, u32[]{:S(2)}, u32[]{:S(2)}) collective-permute-start(bf16[16,3584]{1,0:T(8,128)(2,1)S(1)} %get-tuple-element.32), channel_id=1, source_target_pairs={{0,6},{1,7},{2,4},{3,5},{4,2},{5,3},{6,0},{7,1},{8,14},{9,15},{10,... | collective-permute-start | bytes 344072 | tf_op jit(solution)/shard_map/ppermute | solution.py:46
  16.8 9.5 %collective-permute-start.3 = (bf16[16,3584]{1,0:T(8,128)(2,1)S(1)}, bf16[16,3584]{1,0:T(8,128)(2,1)S(1)}, u32[]{:S(2)}, u32[]{:S(2)}) collective-permute-start(bf16[16,3584]{1,0:T(8,128)(2,1)S(1)} %get-tuple-element.32), channel_id=1, source_target_pairs={{0,4},{1,5},{2,6},{3,7},{4,0},{5,1},{6,2},{7,3},{8,12},{9,13},{10,... | collective-permute-start | bytes 344072 | tf_op jit(solution)/shard_map/ppermute | solution.py:46
  26.6 5.2 %collective-permute-start.4 = (bf16[16,3584]{1,0:T(8,128)(2,1)S(1)}, bf16[16,3584]{1,0:T(8,128)(2,1)S(1)}, u32[]{:S(2)}, u32[]{:S(2)}) collective-permute-start(bf16[16,3584]{1,0:T(8,128)(2,1)S(1)} %shard_map.142.refs_0_), channel_id=1, source_target_pairs={{0,16},{1,17},{2,18},{3,19},{4,20},{5,21},{6,22},{7,23},{8,24},{9,... | collective-permute-start | bytes 344072 | tf_op jit(solution)/shard_map/ppermute | solution.py:46
  28.2 5.0 %collective-permute-start.5 = (bf16[16,3584]{1,0:T(8,128)(2,1)S(1)}, bf16[16,3584]{1,0:T(8,128)(2,1)S(1)}, u32[]{:S(2)}, u32[]{:S(2)}) collective-permute-start(bf16[16,3584]{1,0:T(8,128)(2,1)S(1)} %shard_map.142.refs_0_), channel_id=1, source_target_pairs={{0,1},{1,0},{2,3},{3,2},{4,5},{5,4},{6,7},{7,6},{8,9},{9,8},{10,11... | collective-permute-start | bytes 344072 | tf_op jit(solution)/shard_map/ppermute | solution.py:46
  29.7 5.7 %collective-permute-start.6 = (bf16[16,3584]{1,0:T(8,128)(2,1)S(1)}, bf16[16,3584]{1,0:T(8,128)(2,1)S(1)}, u32[]{:S(2)}, u32[]{:S(2)}) collective-permute-start(bf16[16,3584]{1,0:T(8,128)(2,1)S(1)} %shard_map.142.refs_0_), channel_id=1, source_target_pairs={{0,17},{1,16},{2,19},{3,18},{4,21},{5,20},{6,23},{7,22},{8,25},{9,... | collective-permute-start | bytes 344072 | tf_op jit(solution)/shard_map/ppermute | solution.py:46
  35.4 1.9 %collective-permute-start.7 = (bf16[2,2,16,3584]{3,2,1,0:T(8,128)(2,1)S(1)}, bf16[2,2,16,3584]{3,2,1,0:T(8,128)(2,1)S(1)}, u32[]{:S(2)}, u32[]{:S(2)}) collective-permute-start(bf16[2,2,16,3584]{3,2,1,0:T(8,128)(2,1)S(1)} %shard_map.143.mine_ref.clean_ref), channel_id=1, source_target_pairs={{0,8},{1,9},{2,10},{3,11},{4,12},{5,13},{6,14},{7,15},{8,0},{9,1},... | collective-permute-start | bytes 1376264 | tf_op jit(solution)/shard_map/ppermute | solution.py:46
  40.8 1.8 %collective-permute-start.9 = (bf16[2,32,1792]{2,1,0:T(8,128)(2,1)S(1)}, bf16[2,32,1792]{2,1,0:T(8,128)(2,1)S(1)}, u32[]{:S(2)}, u32[]{:S(2)}) collective-permute-start(bf16[2,32,1792]{2,1,0:T(8,128)(2,1)S(1)} %get-tuple-element.39), channel_id=1, source_target_pairs={{0,8},{1,9},{2,10},{3,11},{4,12},{5,13},{6,14},{7,15},{8,0},{9,1},... | collective-permute-start | bytes 688136 | tf_op jit(solution)/shard_map/ppermute | solution.py:46
  42.1 2.6 %collective-permute-start.8 = (bf16[2,32,1792]{2,1,0:T(8,128)(2,1)S(1)}, bf16[2,32,1792]{2,1,0:T(8,128)(2,1)S(1)}, u32[]{:S(2)}, u32[]{:S(2)}) collective-permute-start(bf16[2,32,1792]{2,1,0:T(8,128)(2,1)S(1)} %get-tuple-element.36), channel_id=1, source_target_pairs={{0,8},{1,9},{2,10},{3,11},{4,12},{5,13},{6,14},{7,15},{8,0},{9,1},... | collective-permute-start | bytes 688136 | tf_op jit(solution)/shard_map/ppermute | solution.py:46
  42.6 6.1 %collective-permute-start.10 = (bf16[32,1792]{1,0:T(8,128)(2,1)S(1)}, bf16[32,1792]{1,0:T(8,128)(2,1)S(1)}, u32[]{:S(2)}, u32[]{:S(2)}) collective-permute-start(bf16[32,1792]{1,0:T(8,128)(2,1)S(1)} %get-tuple-element.40), channel_id=1, source_target_pairs={{0,1},{1,0},{2,3},{3,2},{4,5},{5,4},{6,7},{7,6},{8,9},{9,8},{10,11... | collective-permute-start | bytes 344072 | tf_op jit(solution)/shard_map/ppermute | solution.py:46
  43.1 7.2 %collective-permute-start.11 = (bf16[32,1792]{1,0:T(8,128)(2,1)S(1)}, bf16[32,1792]{1,0:T(8,128)(2,1)S(1)}, u32[]{:S(2)}, u32[]{:S(2)}) collective-permute-start(bf16[32,1792]{1,0:T(8,128)(2,1)S(1)} %get-tuple-element.41), channel_id=1, source_target_pairs={{0,17},{1,16},{2,19},{3,18},{4,21},{5,20},{6,23},{7,22},{8,25},{9,... | collective-permute-start | bytes 344072 | tf_op jit(solution)/shard_map/ppermute | solution.py:46
  44.7 7.1 %collective-permute-start.12 = (bf16[32,1792]{1,0:T(8,128)(2,1)S(1)}, bf16[32,1792]{1,0:T(8,128)(2,1)S(1)}, u32[]{:S(2)}, u32[]{:S(2)}) collective-permute-start(bf16[32,1792]{1,0:T(8,128)(2,1)S(1)} %get-tuple-element.42), channel_id=1, source_target_pairs={{0,16},{1,17},{2,18},{3,19},{4,20},{5,21},{6,22},{7,23},{8,24},{9,... | collective-permute-start | bytes 344072 | tf_op jit(solution)/shard_map/ppermute | solution.py:46
  51.9 13.5 %slice-start.8 = ((s8[12845056]{0:T(1024)(128)(4,1)}), s8[4194304]{0:T(1024)(128)(4,1)S(1)}, s32[]{:S(2)}) async-start(s8[12845056]{0:T(1024)(128)(4,1)} %bitcast.9), calls=%async_computation.8 | async-start | bytes 8388608
  51.9 13.5 %slice-start.9 = ((s8[12845056]{0:T(1024)(128)(4,1)}), s8[4194304]{0:T(1024)(128)(4,1)S(1)}, s32[]{:S(2)}) async-start(s8[12845056]{0:T(1024)(128)(4,1)} %bitcast.9), calls=%async_computation.9 | async-start | bytes 8388608
  51.9 13.5 %slice-start.10 = ((s8[12845056]{0:T(1024)(128)(4,1)}), s8[4194304]{0:T(1024)(128)(4,1)S(1)}, s32[]{:S(2)}) async-start(s8[12845056]{0:T(1024)(128)(4,1)} %bitcast.9), calls=%async_computation.10 | async-start | bytes 8388608
  51.9 13.5 %slice-start.12 = ((s8[12845056]{0:T(1024)(128)(4,1)}), s8[4194304]{0:T(1024)(128)(4,1)S(1)}, s32[]{:S(2)}) async-start(s8[12845056]{0:T(1024)(128)(4,1)} %bitcast.11), calls=%async_computation.12 | async-start | bytes 8388608
  51.9 13.5 %slice-start.13 = ((s8[12845056]{0:T(1024)(128)(4,1)}), s8[4194304]{0:T(1024)(128)(4,1)S(1)}, s32[]{:S(2)}) async-start(s8[12845056]{0:T(1024)(128)(4,1)} %bitcast.11), calls=%async_computation.13 | async-start | bytes 8388608
  52.0 6.1 %collective-permute-start.13 = (bf16[32,1792]{1,0:T(8,128)(2,1)S(1)}, bf16[32,1792]{1,0:T(8,128)(2,1)S(1)}, u32[]{:S(2)}, u32[]{:S(2)}) collective-permute-start(bf16[32,1792]{1,0:T(8,128)(2,1)S(1)} %get-tuple-element.44), channel_id=1, source_target_pairs={{0,2},{1,3},{2,0},{3,1},{4,6},{5,7},{6,4},{7,5},{8,10},{9,11},{10,... | collective-permute-start | bytes 344072 | tf_op jit(solution)/shard_map/ppermute | solution.py:46
  52.1 11.8 %collective-permute-start.14 = (bf16[32,1792]{1,0:T(8,128)(2,1)S(1)}, bf16[32,1792]{1,0:T(8,128)(2,1)S(1)}, u32[]{:S(2)}, u32[]{:S(2)}) collective-permute-start(bf16[32,1792]{1,0:T(8,128)(2,1)S(1)} %get-tuple-element.44), channel_id=1, source_target_pairs={{0,4},{1,5},{2,6},{3,7},{4,0},{5,1},{6,2},{7,3},{8,12},{9,13},{10,... | collective-permute-start | bytes 344072 | tf_op jit(solution)/shard_map/ppermute | solution.py:46
  55.3 8.6 %collective-permute-start.15 = (bf16[32,1792]{1,0:T(8,128)(2,1)S(1)}, bf16[32,1792]{1,0:T(8,128)(2,1)S(1)}, u32[]{:S(2)}, u32[]{:S(2)}) collective-permute-start(bf16[32,1792]{1,0:T(8,128)(2,1)S(1)} %get-tuple-element.44), channel_id=1, source_target_pairs={{0,6},{1,7},{2,4},{3,5},{4,2},{5,3},{6,0},{7,1},{8,14},{9,15},{10,... | collective-permute-start | bytes 344072 | tf_op jit(solution)/shard_map/ppermute | solution.py:46
  64.0 4.9 %collective-permute-start.16 = (bf16[32,1792]{1,0:T(8,128)(2,1)S(1)}, bf16[32,1792]{1,0:T(8,128)(2,1)S(1)}, u32[]{:S(2)}, u32[]{:S(2)}) collective-permute-start(bf16[32,1792]{1,0:T(8,128)(2,1)S(1)} %shard_map.149.recon_ref), channel_id=1, source_target_pairs={{0,1},{1,0},{2,3},{3,2},{4,5},{5,4},{6,7},{7,6},{8,9},{9,8},{10,11... | collective-permute-start | bytes 344072 | tf_op jit(solution)/shard_map/ppermute | solution.py:46
  73.5 7.6 %collective-permute-start.17 = (bf16[64,896]{1,0:T(8,128)(2,1)S(1)}, bf16[64,896]{1,0:T(8,128)(2,1)S(1)}, u32[]{:S(2)}, u32[]{:S(2)}) collective-permute-start(bf16[64,896]{1,0:T(8,128)(2,1)S(1)} %get-tuple-element.51), channel_id=1, source_target_pairs={{0,6},{1,7},{2,4},{3,5},{4,2},{5,3},{6,0},{7,1},{8,14},{9,15},{10,... | collective-permute-start | bytes 344072 | tf_op jit(solution)/shard_map/ppermute | solution.py:46
  75.9 8.9 %collective-permute-start.18 = (bf16[64,896]{1,0:T(8,128)(2,1)S(1)}, bf16[64,896]{1,0:T(8,128)(2,1)S(1)}, u32[]{:S(2)}, u32[]{:S(2)}) collective-permute-start(bf16[64,896]{1,0:T(8,128)(2,1)S(1)} %get-tuple-element.52), channel_id=1, source_target_pairs={{0,4},{1,5},{2,6},{3,7},{4,0},{5,1},{6,2},{7,3},{8,12},{9,13},{10,... | collective-permute-start | bytes 344072 | tf_op jit(solution)/shard_map/ppermute | solution.py:46
  76.8 8.0 %collective-permute-start.19 = (bf16[64,896]{1,0:T(8,128)(2,1)S(1)}, bf16[64,896]{1,0:T(8,128)(2,1)S(1)}, u32[]{:S(2)}, u32[]{:S(2)}) collective-permute-start(bf16[64,896]{1,0:T(8,128)(2,1)S(1)} %get-tuple-element.53), channel_id=1, source_target_pairs={{0,2},{1,3},{2,0},{3,1},{4,6},{5,7},{6,4},{7,5},{8,10},{9,11},{10,... | collective-permute-start | bytes 344072 | tf_op jit(solution)/shard_map/ppermute | solution.py:46
  84.8 4.9 %collective-permute-start.20 = (bf16[64,896]{1,0:T(8,128)(2,1)S(1)}, bf16[64,896]{1,0:T(8,128)(2,1)S(1)}, u32[]{:S(2)}, u32[]{:S(2)}) collective-permute-start(bf16[64,896]{1,0:T(8,128)(2,1)S(1)} %shard_map.153), channel_id=1, source_target_pairs={{0,1},{1,0},{2,3},{3,2},{4,5},{5,4},{6,7},{7,6},{8,9},{9,8},{10,11... | collective-permute-start | bytes 344072 | tf_op jit(solution)/shard_map/ppermute | solution.py:46
  89.8 4.3 %collective-permute-start.23 = (f32[1,64]{1,0:T(1,128)S(1)}, f32[1,64]{1,0:T(1,128)S(1)}, u32[]{:S(2)}, u32[]{:S(2)}) collective-permute-start(f32[1,64]{1,0:T(1,128)S(1)} %bitcast.16), channel_id=1, source_target_pairs={{0,2},{1,3},{2,0},{3,1},{4,6},{5,7},{6,4},{7,5},{8,10},{9,11},{10,... | collective-permute-start | bytes 776 | tf_op jit(solution)/shard_map/ppermute | solution.py:46
  89.9 5.4 %collective-permute-start.22 = (f32[1,64]{1,0:T(1,128)S(1)}, f32[1,64]{1,0:T(1,128)S(1)}, u32[]{:S(2)}, u32[]{:S(2)}) collective-permute-start(f32[1,64]{1,0:T(1,128)S(1)} %bitcast.17), channel_id=1, source_target_pairs={{0,6},{1,7},{2,4},{3,5},{4,2},{5,3},{6,0},{7,1},{8,14},{9,15},{10,... | collective-permute-start | bytes 776 | tf_op jit(solution)/shard_map/ppermute | solution.py:46
  92.6 4.5 %collective-permute-start.21 = (f32[1,64]{1,0:T(1,128)S(1)}, f32[1,64]{1,0:T(1,128)S(1)}, u32[]{:S(2)}, u32[]{:S(2)}) collective-permute-start(f32[1,64]{1,0:T(1,128)S(1)} %bitcast.18), channel_id=1, source_target_pairs={{0,4},{1,5},{2,6},{3,7},{4,0},{5,1},{6,2},{7,3},{8,12},{9,13},{10,... | collective-permute-start | bytes 776 | tf_op jit(solution)/shard_map/ppermute | solution.py:46
  (16 other events, 151.3 us)
where the time goes:
time: 98.1 us; the launch traced here: 97.9 us
  waiting for transfers between devices  47 us (48%)
  starting transfers between devices  30.3 us (31%)
  Pallas kernels  17.7 us (18%)
  between operations  1.06 us (1%)
    ppermute x24, waiting for transfers between devices, swap(): return lax.ppermute(value, AXES, [(i, i ^ mask) for i in range(total)])  47 us
    ppermute x24, starting transfers between devices, swap(): return lax.ppermute(value, AXES, [(i, i ^ mask) for i in range(total)])  30.3 us
    pallas_call x14, Pallas kernels, stage(): pl.pallas_call(kernel, out_shape=[shape(*out) for out in outs], in_specs=...  17.7 us
  transfers between devices with their start and end apart: 24, of which 19 were waited for; matrix products, arithmetic and copies ran while one was open for 1% of the time, Pallas kernels for 4%

commit v1 on v0

--- a/solution.py
+++ b/solution.py
@@ -274,9 +274,9 @@
     core_unit, lane_unit, near_unit, far_unit = n_shard, 2 * n_shard, 1, 2
     plain = list(range(1, n_far))
     first_fars, recon_fars, fars, stat_fars = (
-        ([1, 3, 2], [1, 2, 3], [3, 2, 1], [1, 3, 2]) if n_far == 4 else (plain,) * 4
-    )
-    blocks = [(k, j) for j in range(2) for k in range(n_lane) if k or j]
+        ([3, 2, 1], [1, 2, 3], [3, 2, 1], [1, 3, 2]) if n_far == 4 else (plain,) * 4
+    )
+    blocks = [(k, j) for j in (1, 0) for k in reversed(range(n_lane)) if k or j]
     block_units = [k * lane_unit + j * near_unit for k, j in blocks]
     gain_one, dec_bias, gain_pre, enc_bias = (
         v.reshape(1, -1) for v in (gain_one, dec_bias, gain_pre, enc_bias)
@@ -315,16 +315,16 @@
         limit=8, flops=rows * latent * width, size=latent * width,
     )
     part = (group, half)
-    lanes = list(range(n_lane))
+    outer = list(reversed(range(n_lane)))
     outward = stage(
-        partial(blocks_kernel, lanes), [kept, swap(sent, core_unit)],
+        partial(blocks_kernel, outer), [kept, swap(sent, core_unit)],
         [(part, BF)] * n_lane, 4, scratch=[pltpu.VMEM(mine_half, F32)],
     )
     own, *inward = stage(
-        partial(blocks_kernel, lanes), [kept_near, swap(sent_near, core_unit)],
+        partial(blocks_kernel, range(n_lane)), [kept_near, swap(sent_near, core_unit)],
         [(part, F32)] + [(part, BF)] * (n_lane - 1), 4, scratch=[pltpu.VMEM(mine_half, F32)],
     )
-    got = [swap(v, k * lane_unit + near_unit) for k, v in enumerate(outward)]
+    got = [swap(v, k * lane_unit + near_unit) for k, v in zip(outer, outward)]
     got += [swap(v, k * lane_unit) for k, v in enumerate(inward, 1)]
     total, sent = stage(partial(total_kernel, len(got)), [own] + got, [(part, F32), (part, BF)], 12)
     (recon_near,) = stage(

time: 98.1 us -> 95.6 us (0.975)
  waiting for transfers between devices: 47 us -> 44 us
    ppermute x24, waiting for transfers between devices: 47 us -> 44 us  [swap(): return lax.ppermute(value, AXES, [(i, i ^ mask) for i in range(total)])]
  transfers between devices with their start and end apart: 24 -> 24, of which waited for: 19 -> 18; matrix products, arithmetic and copies ran while one was open for 1% -> 1% of each run, Pallas kernels for 4% -> 4%
where the time goes in v1:
time: 95.6 us; the launch traced here: 95.4 us
  waiting for transfers between devices  44 us (46%)
  starting transfers between devices  30.8 us (32%)
  Pallas kernels  17.7 us (19%)
  between operations  1.06 us (1%)
    ppermute x24, waiting for transfers between devices, swap(): return lax.ppermute(value, AXES, [(i, i ^ mask) for i in range(total)])  44 us
    ppermute x24, starting transfers between devices, swap(): return lax.ppermute(value, AXES, [(i, i ^ mask) for i in range(total)])  30.8 us
    pallas_call x14, Pallas kernels, stage(): pl.pallas_call(kernel, out_shape=[shape(*out) for out in outs], in_specs=...  17.7 us
  transfers between devices with their start and end apart: 24, of which 18 were waited for; matrix products, arithmetic and copies ran while one was open for 1% of the time, Pallas kernels for 4%

profile of v1, /device:TPU:0, one launch (start us, length us, event | category | flops | bytes accessed | tf_op | source)
XLA Modules:
  0.0 95.4 jit_solution(5008207530418109196)
XLA Ops:
  0.6 5.6 %shard_map.140 = (f32[16,3584]{1,0:T(8,128)S(1)}, bf16[16,3584]{1,0:T(8,128)(2,1)S(1)}, f32[16,3584]{1,0:T(8,128)S(1)}) custom-call(bf16[32,1792]{1,0:T(8,128)(2,1)} %x_hbm.1, bf16[1792,3584]{1,0:T(8,128)(2,1)} %w_hbm.1, bf16[32,3584]{1,0:T(8,128)(2,1)} %resid_hbm.1), custom_call_target="tpu_custom_call" | custom-call | flops 5911042048 | bytes 27845056 | tf_op jit(solution)/shard_map/pallas_call | solution.py:29
  6.2 3.0 %collective-permute-start = (bf16[16,3584]{1,0:T(8,128)(2,1)S(1)}, bf16[16,3584]{1,0:T(8,128)(2,1)S(1)}, u32[]{:S(2)}, u32[]{:S(2)}) collective-permute-start(bf16[16,3584]{1,0:T(8,128)(2,1)S(1)} %get-tuple-element.29), channel_id=1, source_target_pairs={{0,1},{1,0},{2,3},{3,2},{4,5},{5,4},{6,7},{7,6},{8,9},{9,8},{10,11... | collective-permute-start | bytes 344072 | tf_op jit(solution)/shard_map/ppermute | solution.py:46
  9.3 3.1 %collective-permute-done.refs_0_ = bf16[16,3584]{1,0:T(8,128)(2,1)S(1)} collective-permute-done((bf16[16,3584]{1,0:T(8,128)(2,1)S(1)}, bf16[16,3584]{1,0:T(8,128)(2,1)S(1)}, u32[]{:S(2)}, u32[]{:S(2)}) %collective-permute-start) | collective-permute-done | bytes 114720 | tf_op jit(solution)/shard_map/ppermute | solution.py:46
  12.5 3.9 %collective-permute-start.1 = (bf16[16,3584]{1,0:T(8,128)(2,1)S(1)}, bf16[16,3584]{1,0:T(8,128)(2,1)S(1)}, u32[]{:S(2)}, u32[]{:S(2)}) collective-permute-start(bf16[16,3584]{1,0:T(8,128)(2,1)S(1)} %get-tuple-element.32), channel_id=1, source_target_pairs={{0,6},{1,7},{2,4},{3,5},{4,2},{5,3},{6,0},{7,1},{8,14},{9,15},{10,... | collective-permute-start | bytes 344072 | tf_op jit(solution)/shard_map/ppermute | solution.py:46
  17.1 3.3 %collective-permute-done.1.refs_0_ = bf16[16,3584]{1,0:T(8,128)(2,1)S(1)} collective-permute-done((bf16[16,3584]{1,0:T(8,128)(2,1)S(1)}, bf16[16,3584]{1,0:T(8,128)(2,1)S(1)}, u32[]{:S(2)}, u32[]{:S(2)}) %collective-permute-start.1) | collective-permute-done | bytes 114720 | tf_op jit(solution)/shard_map/ppermute | solution.py:46
  20.3 4.9 %collective-permute-done.2.refs_1_ = bf16[16,3584]{1,0:T(8,128)(2,1)S(1)} collective-permute-done((bf16[16,3584]{1,0:T(8,128)(2,1)S(1)}, bf16[16,3584]{1,0:T(8,128)(2,1)S(1)}, u32[]{:S(2)}, u32[]{:S(2)}) %collective-permute-start.2) | collective-permute-done | bytes 114720 | tf_op jit(solution)/shard_map/ppermute | solution.py:46
  25.5 2.5 %collective-permute-start.4 = (bf16[16,3584]{1,0:T(8,128)(2,1)S(1)}, bf16[16,3584]{1,0:T(8,128)(2,1)S(1)}, u32[]{:S(2)}, u32[]{:S(2)}) collective-permute-start(bf16[16,3584]{1,0:T(8,128)(2,1)S(1)} %shard_map.142.refs_0_), channel_id=1, source_target_pairs={{0,17},{1,16},{2,19},{3,18},{4,21},{5,20},{6,23},{7,22},{8,25},{9,... | collective-permute-start | bytes 344072 | tf_op jit(solution)/shard_map/ppermute | solution.py:46
  29.0 3.0 %collective-permute-done.4.refs_1_ = bf16[16,3584]{1,0:T(8,128)(2,1)S(1)} collective-permute-done((bf16[16,3584]{1,0:T(8,128)(2,1)S(1)}, bf16[16,3584]{1,0:T(8,128)(2,1)S(1)}, u32[]{:S(2)}, u32[]{:S(2)}) %collective-permute-start.4) | collective-permute-done | bytes 114720 | tf_op jit(solution)/shard_map/ppermute | solution.py:46
  32.0 1.2 %collective-permute-done.5.refs_2_ = bf16[16,3584]{1,0:T(8,128)(2,1)S(1)} collective-permute-done((bf16[16,3584]{1,0:T(8,128)(2,1)S(1)}, bf16[16,3584]{1,0:T(8,128)(2,1)S(1)}, u32[]{:S(2)}, u32[]{:S(2)}) %collective-permute-start.5) | collective-permute-done | bytes 114720 | tf_op jit(solution)/shard_map/ppermute | solution.py:46
  33.6 1.8 %collective-permute-done.7.theirs_ref = bf16[2,2,16,3584]{3,2,1,0:T(8,128)(2,1)S(1)} collective-permute-done((bf16[2,2,16,3584]{3,2,1,0:T(8,128)(2,1)S(1)}, bf16[2,2,16,3584]{3,2,1,0:T(8,128)(2,1)S(1)}, u32[]{:S(2)}, u32[]{:S(2)}) %collective-permute-start.7) | collective-permute-done | bytes 458784 | tf_op jit(solution)/shard_map/ppermute | solution.py:46
  35.4 3.4 %shard_map.144 = (bf16[128,2048]{1,0:T(8,128)(2,1)}, bf16[128,2048]{1,0:T(8,128)(2,1)S(1)}, f32[2,32,1792]{2,1,0:T(8,128)S(1)}, bf16[2,32,1792]{2,1,0:T(8,128)(2,1)S(1)}) custom-call(bf16[2,2,16,3584]{3,2,1,0:T(8,128)(2,1)S(1)} %shard_map.143.mine_ref.clean_ref, bf16[2,2,16,3584]{3,2,1,0:T(8,128)(2,1)S(1)} %collective-permute-done.7.theirs_ref, ...), custom_call_target="tpu_custom_call" | custom-call | flops 5018572288 | bytes 28020096 | tf_op jit(solution)/shard_map/pallas_call | solution.py:29
  39.0 1.1 %shard_map.145 = (f32[2,32,1792]{2,1,0:T(8,128)S(1)}, bf16[2,32,1792]{2,1,0:T(8,128)(2,1)S(1)}) custom-call(bf16[128,2048]{1,0:T(8,128)(2,1)S(1)} %get-tuple-element.34.hold_ref, bf16[2048,3584]{1,0:T(8,128)(2,1)S(1)} %bitcast.8), custom_call_target="tpu_custom_call" | custom-call | flops 3139524096 | bytes 13340032 | tf_op jit(solution)/shard_map/pallas_call | solution.py:29
  40.7 2.1 %collective-permute-start.10 = (bf16[32,1792]{1,0:T(8,128)(2,1)S(1)}, bf16[32,1792]{1,0:T(8,128)(2,1)S(1)}, u32[]{:S(2)}, u32[]{:S(2)}) collective-permute-start(bf16[32,1792]{1,0:T(8,128)(2,1)S(1)} %get-tuple-element.40), channel_id=1, source_target_pairs={{0,17},{1,16},{2,19},{3,18},{4,21},{5,20},{6,23},{7,22},{8,25},{9,... | collective-permute-start | bytes 344072 | tf_op jit(solution)/shard_map/ppermute | solution.py:46
  44.4 3.3 %collective-permute-done.10.refs_0_ = bf16[32,1792]{1,0:T(8,128)(2,1)S(1)} collective-permute-done((bf16[32,1792]{1,0:T(8,128)(2,1)S(1)}, bf16[32,1792]{1,0:T(8,128)(2,1)S(1)}, u32[]{:S(2)}, u32[]{:S(2)}) %collective-permute-start.10) | collective-permute-done | bytes 114720 | tf_op jit(solution)/shard_map/ppermute | solution.py:46
  47.6 1.4 %collective-permute-done.11.refs_1_ = bf16[32,1792]{1,0:T(8,128)(2,1)S(1)} collective-permute-done((bf16[32,1792]{1,0:T(8,128)(2,1)S(1)}, bf16[32,1792]{1,0:T(8,128)(2,1)S(1)}, u32[]{:S(2)}, u32[]{:S(2)}) %collective-permute-start.11) | collective-permute-done | bytes 114720 | tf_op jit(solution)/shard_map/ppermute | solution.py:46
  49.6 2.9 %collective-permute-start.14 = (bf16[32,1792]{1,0:T(8,128)(2,1)S(1)}, bf16[32,1792]{1,0:T(8,128)(2,1)S(1)}, u32[]{:S(2)}, u32[]{:S(2)}) collective-permute-start(bf16[32,1792]{1,0:T(8,128)(2,1)S(1)} %get-tuple-element.44), channel_id=1, source_target_pairs={{0,4},{1,5},{2,6},{3,7},{4,0},{5,1},{6,2},{7,3},{8,12},{9,13},{10,... | collective-permute-start | bytes 344072 | tf_op jit(solution)/shard_map/ppermute | solution.py:46
  52.4 1.4 %collective-permute-start.15 = (bf16[32,1792]{1,0:T(8,128)(2,1)S(1)}, bf16[32,1792]{1,0:T(8,128)(2,1)S(1)}, u32[]{:S(2)}, u32[]{:S(2)}) collective-permute-start(bf16[32,1792]{1,0:T(8,128)(2,1)S(1)} %get-tuple-element.44), channel_id=1, source_target_pairs={{0,6},{1,7},{2,4},{3,5},{4,2},{5,3},{6,0},{7,1},{8,14},{9,15},{10,... | collective-permute-start | bytes 344072 | tf_op jit(solution)/shard_map/ppermute | solution.py:46
  53.9 1.9 %collective-permute-done.13.refs_0_ = bf16[32,1792]{1,0:T(8,128)(2,1)S(1)} collective-permute-done((bf16[32,1792]{1,0:T(8,128)(2,1)S(1)}, bf16[32,1792]{1,0:T(8,128)(2,1)S(1)}, u32[]{:S(2)}, u32[]{:S(2)}) %collective-permute-start.13) | collective-permute-done | bytes 114720 | tf_op jit(solution)/shard_map/ppermute | solution.py:46
  55.8 5.6 %collective-permute-done.14.refs_1_ = bf16[32,1792]{1,0:T(8,128)(2,1)S(1)} collective-permute-done((bf16[32,1792]{1,0:T(8,128)(2,1)S(1)}, bf16[32,1792]{1,0:T(8,128)(2,1)S(1)}, u32[]{:S(2)}, u32[]{:S(2)}) %collective-permute-start.14) | collective-permute-done | bytes 114720 | tf_op jit(solution)/shard_map/ppermute | solution.py:46
  61.5 1.5 %collective-permute-start.16 = (bf16[32,1792]{1,0:T(8,128)(2,1)S(1)}, bf16[32,1792]{1,0:T(8,128)(2,1)S(1)}, u32[]{:S(2)}, u32[]{:S(2)}) collective-permute-start(bf16[32,1792]{1,0:T(8,128)(2,1)S(1)} %shard_map.149.recon_ref), channel_id=1, source_target_pairs={{0,1},{1,0},{2,3},{3,2},{4,5},{5,4},{6,7},{7,6},{8,9},{9,8},{10,11... | collective-permute-start | bytes 344072 | tf_op jit(solution)/shard_map/ppermute | solution.py:46
  63.1 2.4 %shard_map.150 = (f32[64,1792]{1,0:T(8,128)S(1)}, f32[64,1792]{1,0:T(8,128)S(1)}) custom-call(bf16[2,2,16,3584]{3,2,1,0:T(8,128)(2,1)S(1)} %shard_map.143.mine_ref.clean_ref, bf16[32,1792]{1,0:T(8,128)(2,1)S(1)} %shard_map.149.recon_ref, f32[1,3584]{1,0:T(1,128)S(1)} %reshape.40.gain_ref, bf16[3584,1792]{1,0:T(8,128)(2,1)S(1)} %bitcast.10, ...), custom_call_target="tpu_custom_call" | custom-call | flops 822083584 | bytes 12845056 | tf_op jit(solution)/shard_map/pallas_call | solution.py:29
  66.3 2.9 %shard_map.151 = (f32[64,3584]{1,0:T(8,128)S(1)}, bf16[64,1792]{1,0:T(8,128)(2,1)S(1)}, bf16[64,896]{1,0:T(8,128)(2,1)S(1)}) custom-call(bf16[2,2,16,3584]{3,2,1,0:T(8,128)(2,1)S(1)} %shard_map.143.mine_ref.clean_ref, bf16[32,1792]{1,0:T(8,128)(2,1)S(1)} %shard_map.149.recon_ref, bf16[32,1792]{1,0:T(8,128)(2,1)S(1)} %collective-permute-done.16.got_ref, ...), custom_call_target="tpu_custom_call" | custom-call | flops 1233125376 | bytes 19267584 | tf_op jit(solution)/shard_map/pallas_call | solution.py:29
  69.3 1.7 %shard_map.152 = (bf16[64,896]{1,0:T(8,128)(2,1)S(1)}, bf16[64,896]{1,0:T(8,128)(2,1)S(1)}, f32[64,896]{1,0:T(8,128)S(1)}) custom-call(bf16[64,1792]{1,0:T(8,128)(2,1)S(1)} %get-tuple-element.49.act_ref, bf16[1792,3584]{1,0:T(8,128)(2,1)S(1)} %bitcast.6), custom_call_target="tpu_custom_call" | custom-call | flops 411041792 | bytes 6422528 | tf_op jit(solution)/shard_map/pallas_call | solution.py:29
  71.0 2.4 %collective-permute-start.17 = (bf16[64,896]{1,0:T(8,128)(2,1)S(1)}, bf16[64,896]{1,0:T(8,128)(2,1)S(1)}, u32[]{:S(2)}, u32[]{:S(2)}) collective-permute-start(bf16[64,896]{1,0:T(8,128)(2,1)S(1)} %get-tuple-element.51), channel_id=1, source_target_pairs={{0,6},{1,7},{2,4},{3,5},{4,2},{5,3},{6,0},{7,1},{8,14},{9,15},{10,... | collective-permute-start | bytes 344072 | tf_op jit(solution)/shard_map/ppermute | solution.py:46
  74.3 1.1 %collective-permute-start.19 = (bf16[64,896]{1,0:T(8,128)(2,1)S(1)}, bf16[64,896]{1,0:T(8,128)(2,1)S(1)}, u32[]{:S(2)}, u32[]{:S(2)}) collective-permute-start(bf16[64,896]{1,0:T(8,128)(2,1)S(1)} %get-tuple-element.53), channel_id=1, source_target_pairs={{0,2},{1,3},{2,0},{3,1},{4,6},{5,7},{6,4},{7,5},{8,10},{9,11},{10,... | collective-permute-start | bytes 344072 | tf_op jit(solution)/shard_map/ppermute | solution.py:46
  75.4 3.3 %collective-permute-done.17.refs_0_ = bf16[64,896]{1,0:T(8,128)(2,1)S(1)} collective-permute-done((bf16[64,896]{1,0:T(8,128)(2,1)S(1)}, bf16[64,896]{1,0:T(8,128)(2,1)S(1)}, u32[]{:S(2)}, u32[]{:S(2)}) %collective-permute-start.17) | collective-permute-done | bytes 114720 | tf_op jit(solution)/shard_map/ppermute | solution.py:46
  78.7 3.6 %collective-permute-done.18.refs_1_ = bf16[64,896]{1,0:T(8,128)(2,1)S(1)} collective-permute-done((bf16[64,896]{1,0:T(8,128)(2,1)S(1)}, bf16[64,896]{1,0:T(8,128)(2,1)S(1)}, u32[]{:S(2)}, u32[]{:S(2)}) %collective-permute-start.18) | collective-permute-done | bytes 114720 | tf_op jit(solution)/shard_map/ppermute | solution.py:46
  82.4 1.5 %collective-permute-start.20 = (bf16[64,896]{1,0:T(8,128)(2,1)S(1)}, bf16[64,896]{1,0:T(8,128)(2,1)S(1)}, u32[]{:S(2)}, u32[]{:S(2)}) collective-permute-start(bf16[64,896]{1,0:T(8,128)(2,1)S(1)} %shard_map.153), channel_id=1, source_target_pairs={{0,1},{1,0},{2,3},{3,2},{4,5},{5,4},{6,7},{7,6},{8,9},{9,8},{10,11... | collective-permute-start | bytes 344072 | tf_op jit(solution)/shard_map/ppermute | solution.py:46
  83.8 3.4 %collective-permute-done.20 = bf16[64,896]{1,0:T(8,128)(2,1)S(1)} collective-permute-done((bf16[64,896]{1,0:T(8,128)(2,1)S(1)}, bf16[64,896]{1,0:T(8,128)(2,1)S(1)}, u32[]{:S(2)}, u32[]{:S(2)}) %collective-permute-start.20) | collective-permute-done | bytes 114720 | tf_op jit(solution)/shard_map/ppermute | solution.py:46
  87.4 2.7 %collective-permute-start.22 = (f32[1,64]{1,0:T(1,128)S(1)}, f32[1,64]{1,0:T(1,128)S(1)}, u32[]{:S(2)}, u32[]{:S(2)}) collective-permute-start(f32[1,64]{1,0:T(1,128)S(1)} %bitcast.17), channel_id=1, source_target_pairs={{0,6},{1,7},{2,4},{3,5},{4,2},{5,3},{6,0},{7,1},{8,14},{9,15},{10,... | collective-permute-start | bytes 776 | tf_op jit(solution)/shard_map/ppermute | solution.py:46
  91.7 1.2 %collective-permute-done.22 = f32[1,64]{1,0:T(1,128)S(1)} collective-permute-done((f32[1,64]{1,0:T(1,128)S(1)}, f32[1,64]{1,0:T(1,128)S(1)}, u32[]{:S(2)}, u32[]{:S(2)}) %collective-permute-start.22) | collective-permute-done | bytes 288 | tf_op jit(solution)/shard_map/ppermute | solution.py:46
  92.9 1.7 %collective-permute-done.21 = f32[1,64]{1,0:T(1,128)S(1)} collective-permute-done((f32[1,64]{1,0:T(1,128)S(1)}, f32[1,64]{1,0:T(1,128)S(1)}, u32[]{:S(2)}, u32[]{:S(2)}) %collective-permute-start.21) | collective-permute-done | bytes 288 | tf_op jit(solution)/shard_map/ppermute | solution.py:46
  (91 shorter events, 9.6 us)
Async XLA Ops:
  6.2 6.2 %collective-permute-start = (bf16[16,3584]{1,0:T(8,128)(2,1)S(1)}, bf16[16,3584]{1,0:T(8,128)(2,1)S(1)}, u32[]{:S(2)}, u32[]{:S(2)}) collective-permute-start(bf16[16,3584]{1,0:T(8,128)(2,1)S(1)} %get-tuple-element.29), channel_id=1, source_target_pairs={{0,1},{1,0},{2,3},{3,2},{4,5},{5,4},{6,7},{7,6},{8,9},{9,8},{10,11... | collective-permute-start | bytes 344072 | tf_op jit(solution)/shard_map/ppermute | solution.py:46
  12.4 22.9 %slice-start.16 = ((s8[14680064]{0:T(1024)(128)(4,1)}), s8[4194304]{0:T(1024)(128)(4,1)S(1)}, s32[]{:S(2)}) async-start(s8[14680064]{0:T(1024)(128)(4,1)} %bitcast.13), calls=%async_computation.16 | async-start | bytes 8388608
  12.4 22.9 %slice-start.17 = ((s8[14680064]{0:T(1024)(128)(4,1)}), s8[4194304]{0:T(1024)(128)(4,1)S(1)}, s32[]{:S(2)}) async-start(s8[14680064]{0:T(1024)(128)(4,1)} %bitcast.13), calls=%async_computation.17 | async-start | bytes 8388608
  12.4 22.9 %slice-start.18 = ((s8[14680064]{0:T(1024)(128)(4,1)}), s8[4194304]{0:T(1024)(128)(4,1)S(1)}, s32[]{:S(2)}) async-start(s8[14680064]{0:T(1024)(128)(4,1)} %bitcast.13), calls=%async_computation.18 | async-start | bytes 8388608
  12.5 7.8 %collective-permute-start.1 = (bf16[16,3584]{1,0:T(8,128)(2,1)S(1)}, bf16[16,3584]{1,0:T(8,128)(2,1)S(1)}, u32[]{:S(2)}, u32[]{:S(2)}) collective-permute-start(bf16[16,3584]{1,0:T(8,128)(2,1)S(1)} %get-tuple-element.32), channel_id=1, source_target_pairs={{0,6},{1,7},{2,4},{3,5},{4,2},{5,3},{6,0},{7,1},{8,14},{9,15},{10,... | collective-permute-start | bytes 344072 | tf_op jit(solution)/shard_map/ppermute | solution.py:46
  16.4 8.8 %collective-permute-start.2 = (bf16[16,3584]{1,0:T(8,128)(2,1)S(1)}, bf16[16,3584]{1,0:T(8,128)(2,1)S(1)}, u32[]{:S(2)}, u32[]{:S(2)}) collective-permute-start(bf16[16,3584]{1,0:T(8,128)(2,1)S(1)} %get-tuple-element.32), channel_id=1, source_target_pairs={{0,4},{1,5},{2,6},{3,7},{4,0},{5,1},{6,2},{7,3},{8,12},{9,13},{10,... | collective-permute-start | bytes 344072 | tf_op jit(solution)/shard_map/ppermute | solution.py:46
  16.4 8.8 %collective-permute-start.3 = (bf16[16,3584]{1,0:T(8,128)(2,1)S(1)}, bf16[16,3584]{1,0:T(8,128)(2,1)S(1)}, u32[]{:S(2)}, u32[]{:S(2)}) collective-permute-start(bf16[16,3584]{1,0:T(8,128)(2,1)S(1)} %get-tuple-element.32), channel_id=1, source_target_pairs={{0,2},{1,3},{2,0},{3,1},{4,6},{5,7},{6,4},{7,5},{8,10},{9,11},{10,... | collective-permute-start | bytes 344072 | tf_op jit(solution)/shard_map/ppermute | solution.py:46
  25.5 6.5 %collective-permute-start.4 = (bf16[16,3584]{1,0:T(8,128)(2,1)S(1)}, bf16[16,3584]{1,0:T(8,128)(2,1)S(1)}, u32[]{:S(2)}, u32[]{:S(2)}) collective-permute-start(bf16[16,3584]{1,0:T(8,128)(2,1)S(1)} %shard_map.142.refs_0_), channel_id=1, source_target_pairs={{0,17},{1,16},{2,19},{3,18},{4,21},{5,20},{6,23},{7,22},{8,25},{9,... | collective-permute-start | bytes 344072 | tf_op jit(solution)/shard_map/ppermute | solution.py:46
  28.0 5.2 %collective-permute-start.5 = (bf16[16,3584]{1,0:T(8,128)(2,1)S(1)}, bf16[16,3584]{1,0:T(8,128)(2,1)S(1)}, u32[]{:S(2)}, u32[]{:S(2)}) collective-permute-start(bf16[16,3584]{1,0:T(8,128)(2,1)S(1)} %shard_map.142.refs_0_), channel_id=1, source_target_pairs={{0,1},{1,0},{2,3},{3,2},{4,5},{5,4},{6,7},{7,6},{8,9},{9,8},{10,11... | collective-permute-start | bytes 344072 | tf_op jit(solution)/shard_map/ppermute | solution.py:46
  28.5 4.9 %collective-permute-start.6 = (bf16[16,3584]{1,0:T(8,128)(2,1)S(1)}, bf16[16,3584]{1,0:T(8,128)(2,1)S(1)}, u32[]{:S(2)}, u32[]{:S(2)}) collective-permute-start(bf16[16,3584]{1,0:T(8,128)(2,1)S(1)} %shard_map.142.refs_0_), channel_id=1, source_target_pairs={{0,16},{1,17},{2,18},{3,19},{4,20},{5,21},{6,22},{7,23},{8,24},{9,... | collective-permute-start | bytes 344072 | tf_op jit(solution)/shard_map/ppermute | solution.py:46
  33.5 1.9 %collective-permute-start.7 = (bf16[2,2,16,3584]{3,2,1,0:T(8,128)(2,1)S(1)}, bf16[2,2,16,3584]{3,2,1,0:T(8,128)(2,1)S(1)}, u32[]{:S(2)}, u32[]{:S(2)}) collective-permute-start(bf16[2,2,16,3584]{3,2,1,0:T(8,128)(2,1)S(1)} %shard_map.143.mine_ref.clean_ref), channel_id=1, source_target_pairs={{0,8},{1,9},{2,10},{3,11},{4,12},{5,13},{6,14},{7,15},{8,0},{9,1},... | collective-permute-start | bytes 1376264 | tf_op jit(solution)/shard_map/ppermute | solution.py:46
  38.8 1.8 %collective-permute-start.9 = (bf16[2,32,1792]{2,1,0:T(8,128)(2,1)S(1)}, bf16[2,32,1792]{2,1,0:T(8,128)(2,1)S(1)}, u32[]{:S(2)}, u32[]{:S(2)}) collective-permute-start(bf16[2,32,1792]{2,1,0:T(8,128)(2,1)S(1)} %get-tuple-element.39), channel_id=1, source_target_pairs={{0,8},{1,9},{2,10},{3,11},{4,12},{5,13},{6,14},{7,15},{8,0},{9,1},... | collective-permute-start | bytes 688136 | tf_op jit(solution)/shard_map/ppermute | solution.py:46
  40.1 3.3 %collective-permute-start.8 = (bf16[2,32,1792]{2,1,0:T(8,128)(2,1)S(1)}, bf16[2,32,1792]{2,1,0:T(8,128)(2,1)S(1)}, u32[]{:S(2)}, u32[]{:S(2)}) collective-permute-start(bf16[2,32,1792]{2,1,0:T(8,128)(2,1)S(1)} %get-tuple-element.36), channel_id=1, source_target_pairs={{0,8},{1,9},{2,10},{3,11},{4,12},{5,13},{6,14},{7,15},{8,0},{9,1},... | collective-permute-start | bytes 688136 | tf_op jit(solution)/shard_map/ppermute | solution.py:46
  40.7 7.0 %collective-permute-start.10 = (bf16[32,1792]{1,0:T(8,128)(2,1)S(1)}, bf16[32,1792]{1,0:T(8,128)(2,1)S(1)}, u32[]{:S(2)}, u32[]{:S(2)}) collective-permute-start(bf16[32,1792]{1,0:T(8,128)(2,1)S(1)} %get-tuple-element.40), channel_id=1, source_target_pairs={{0,17},{1,16},{2,19},{3,18},{4,21},{5,20},{6,23},{7,22},{8,25},{9,... | collective-permute-start | bytes 344072 | tf_op jit(solution)/shard_map/ppermute | solution.py:46
  42.8 6.2 %collective-permute-start.11 = (bf16[32,1792]{1,0:T(8,128)(2,1)S(1)}, bf16[32,1792]{1,0:T(8,128)(2,1)S(1)}, u32[]{:S(2)}, u32[]{:S(2)}) collective-permute-start(bf16[32,1792]{1,0:T(8,128)(2,1)S(1)} %get-tuple-element.41), channel_id=1, source_target_pairs={{0,1},{1,0},{2,3},{3,2},{4,5},{5,4},{6,7},{7,6},{8,9},{9,8},{10,11... | collective-permute-start | bytes 344072 | tf_op jit(solution)/shard_map/ppermute | solution.py:46
  43.5 5.8 %collective-permute-start.12 = (bf16[32,1792]{1,0:T(8,128)(2,1)S(1)}, bf16[32,1792]{1,0:T(8,128)(2,1)S(1)}, u32[]{:S(2)}, u32[]{:S(2)}) collective-permute-start(bf16[32,1792]{1,0:T(8,128)(2,1)S(1)} %get-tuple-element.42), channel_id=1, source_target_pairs={{0,16},{1,17},{2,18},{3,19},{4,20},{5,21},{6,22},{7,23},{8,24},{9,... | collective-permute-start | bytes 344072 | tf_op jit(solution)/shard_map/ppermute | solution.py:46
  49.3 13.7 %slice-start.8 = ((s8[12845056]{0:T(1024)(128)(4,1)}), s8[4194304]{0:T(1024)(128)(4,1)S(1)}, s32[]{:S(2)}) async-start(s8[12845056]{0:T(1024)(128)(4,1)} %bitcast.9), calls=%async_computation.8 | async-start | bytes 8388608
  49.3 13.7 %slice-start.9 = ((s8[12845056]{0:T(1024)(128)(4,1)}), s8[4194304]{0:T(1024)(128)(4,1)S(1)}, s32[]{:S(2)}) async-start(s8[12845056]{0:T(1024)(128)(4,1)} %bitcast.9), calls=%async_computation.9 | async-start | bytes 8388608
  49.3 13.7 %slice-start.10 = ((s8[12845056]{0:T(1024)(128)(4,1)}), s8[4194304]{0:T(1024)(128)(4,1)S(1)}, s32[]{:S(2)}) async-start(s8[12845056]{0:T(1024)(128)(4,1)} %bitcast.9), calls=%async_computation.10 | async-start | bytes 8388608
  49.3 13.7 %slice-start.12 = ((s8[12845056]{0:T(1024)(128)(4,1)}), s8[4194304]{0:T(1024)(128)(4,1)S(1)}, s32[]{:S(2)}) async-start(s8[12845056]{0:T(1024)(128)(4,1)} %bitcast.11), calls=%async_computation.12 | async-start | bytes 8388608
  49.3 13.7 %slice-start.13 = ((s8[12845056]{0:T(1024)(128)(4,1)}), s8[4194304]{0:T(1024)(128)(4,1)S(1)}, s32[]{:S(2)}) async-start(s8[12845056]{0:T(1024)(128)(4,1)} %bitcast.11), calls=%async_computation.13 | async-start | bytes 8388608
  49.4 6.4 %collective-permute-start.13 = (bf16[32,1792]{1,0:T(8,128)(2,1)S(1)}, bf16[32,1792]{1,0:T(8,128)(2,1)S(1)}, u32[]{:S(2)}, u32[]{:S(2)}) collective-permute-start(bf16[32,1792]{1,0:T(8,128)(2,1)S(1)} %get-tuple-element.44), channel_id=1, source_target_pairs={{0,2},{1,3},{2,0},{3,1},{4,6},{5,7},{6,4},{7,5},{8,10},{9,11},{10,... | collective-permute-start | bytes 344072 | tf_op jit(solution)/shard_map/ppermute | solution.py:46
  49.6 11.8 %collective-permute-start.14 = (bf16[32,1792]{1,0:T(8,128)(2,1)S(1)}, bf16[32,1792]{1,0:T(8,128)(2,1)S(1)}, u32[]{:S(2)}, u32[]{:S(2)}) collective-permute-start(bf16[32,1792]{1,0:T(8,128)(2,1)S(1)} %get-tuple-element.44), channel_id=1, source_target_pairs={{0,4},{1,5},{2,6},{3,7},{4,0},{5,1},{6,2},{7,3},{8,12},{9,13},{10,... | collective-permute-start | bytes 344072 | tf_op jit(solution)/shard_map/ppermute | solution.py:46
  52.4 9.0 %collective-permute-start.15 = (bf16[32,1792]{1,0:T(8,128)(2,1)S(1)}, bf16[32,1792]{1,0:T(8,128)(2,1)S(1)}, u32[]{:S(2)}, u32[]{:S(2)}) collective-permute-start(bf16[32,1792]{1,0:T(8,128)(2,1)S(1)} %get-tuple-element.44), channel_id=1, source_target_pairs={{0,6},{1,7},{2,4},{3,5},{4,2},{5,3},{6,0},{7,1},{8,14},{9,15},{10,... | collective-permute-start | bytes 344072 | tf_op jit(solution)/shard_map/ppermute | solution.py:46
  61.5 4.9 %collective-permute-start.16 = (bf16[32,1792]{1,0:T(8,128)(2,1)S(1)}, bf16[32,1792]{1,0:T(8,128)(2,1)S(1)}, u32[]{:S(2)}, u32[]{:S(2)}) collective-permute-start(bf16[32,1792]{1,0:T(8,128)(2,1)S(1)} %shard_map.149.recon_ref), channel_id=1, source_target_pairs={{0,1},{1,0},{2,3},{3,2},{4,5},{5,4},{6,7},{7,6},{8,9},{9,8},{10,11... | collective-permute-start | bytes 344072 | tf_op jit(solution)/shard_map/ppermute | solution.py:46
  71.0 7.7 %collective-permute-start.17 = (bf16[64,896]{1,0:T(8,128)(2,1)S(1)}, bf16[64,896]{1,0:T(8,128)(2,1)S(1)}, u32[]{:S(2)}, u32[]{:S(2)}) collective-permute-start(bf16[64,896]{1,0:T(8,128)(2,1)S(1)} %get-tuple-element.51), channel_id=1, source_target_pairs={{0,6},{1,7},{2,4},{3,5},{4,2},{5,3},{6,0},{7,1},{8,14},{9,15},{10,... | collective-permute-start | bytes 344072 | tf_op jit(solution)/shard_map/ppermute | solution.py:46
  73.4 8.9 %collective-permute-start.18 = (bf16[64,896]{1,0:T(8,128)(2,1)S(1)}, bf16[64,896]{1,0:T(8,128)(2,1)S(1)}, u32[]{:S(2)}, u32[]{:S(2)}) collective-permute-start(bf16[64,896]{1,0:T(8,128)(2,1)S(1)} %get-tuple-element.52), channel_id=1, source_target_pairs={{0,4},{1,5},{2,6},{3,7},{4,0},{5,1},{6,2},{7,3},{8,12},{9,13},{10,... | collective-permute-start | bytes 344072 | tf_op jit(solution)/shard_map/ppermute | solution.py:46
  74.3 8.0 %collective-permute-start.19 = (bf16[64,896]{1,0:T(8,128)(2,1)S(1)}, bf16[64,896]{1,0:T(8,128)(2,1)S(1)}, u32[]{:S(2)}, u32[]{:S(2)}) collective-permute-start(bf16[64,896]{1,0:T(8,128)(2,1)S(1)} %get-tuple-element.53), channel_id=1, source_target_pairs={{0,2},{1,3},{2,0},{3,1},{4,6},{5,7},{6,4},{7,5},{8,10},{9,11},{10,... | collective-permute-start | bytes 344072 | tf_op jit(solution)/shard_map/ppermute | solution.py:46
  82.4 4.9 %collective-permute-start.20 = (bf16[64,896]{1,0:T(8,128)(2,1)S(1)}, bf16[64,896]{1,0:T(8,128)(2,1)S(1)}, u32[]{:S(2)}, u32[]{:S(2)}) collective-permute-start(bf16[64,896]{1,0:T(8,128)(2,1)S(1)} %shard_map.153), channel_id=1, source_target_pairs={{0,1},{1,0},{2,3},{3,2},{4,5},{5,4},{6,7},{7,6},{8,9},{9,8},{10,11... | collective-permute-start | bytes 344072 | tf_op jit(solution)/shard_map/ppermute | solution.py:46
  87.4 4.3 %collective-permute-start.23 = (f32[1,64]{1,0:T(1,128)S(1)}, f32[1,64]{1,0:T(1,128)S(1)}, u32[]{:S(2)}, u32[]{:S(2)}) collective-permute-start(f32[1,64]{1,0:T(1,128)S(1)} %bitcast.16), channel_id=1, source_target_pairs={{0,2},{1,3},{2,0},{3,1},{4,6},{5,7},{6,4},{7,5},{8,10},{9,11},{10,... | collective-permute-start | bytes 776 | tf_op jit(solution)/shard_map/ppermute | solution.py:46
  87.4 5.4 %collective-permute-start.22 = (f32[1,64]{1,0:T(1,128)S(1)}, f32[1,64]{1,0:T(1,128)S(1)}, u32[]{:S(2)}, u32[]{:S(2)}) collective-permute-start(f32[1,64]{1,0:T(1,128)S(1)} %bitcast.17), channel_id=1, source_target_pairs={{0,6},{1,7},{2,4},{3,5},{4,2},{5,3},{6,0},{7,1},{8,14},{9,15},{10,... | collective-permute-start | bytes 776 | tf_op jit(solution)/shard_map/ppermute | solution.py:46
  90.1 4.5 %collective-permute-start.21 = (f32[1,64]{1,0:T(1,128)S(1)}, f32[1,64]{1,0:T(1,128)S(1)}, u32[]{:S(2)}, u32[]{:S(2)}) collective-permute-start(f32[1,64]{1,0:T(1,128)S(1)} %bitcast.18), channel_id=1, source_target_pairs={{0,4},{1,5},{2,6},{3,7},{4,0},{5,1},{6,2},{7,3},{8,12},{9,13},{10,... | collective-permute-start | bytes 776 | tf_op jit(solution)/shard_map/ppermute | solution.py:46
  (16 other events, 147.2 us)

commit v2 on v1

--- a/solution.py
+++ b/solution.py
@@ -368,8 +368,12 @@
     second_cols = lax.dynamic_slice_in_dim(second, (index % 2) * columns, columns, 1)
     stream_cols = lax.dynamic_slice_in_dim(stream, index * columns, columns, 1)
     post_cols = lax.dynamic_slice_in_dim(gain_post, index * columns, columns, 0)
-    outputs = stream_cols + second_cols * lax.rsqrt(second_sq / width + 1e-06) * post_cols
-    delta = outputs[group:] - outputs[:group]
+    scale = lax.rsqrt(second_sq / width + 1e-06)
+    clean_out, recon_out = (
+        stream_cols[rows] + second_cols[rows] * scale[rows] * post_cols
+        for rows in (slice(None, group), slice(group, None))
+    )
+    delta = recon_out - clean_out
     return (latents, delta)
 
 

time: 95.6 us -> 95.7 us (level)
  no operation moved by 1% of the time
where the time goes in v2:
time: 95.7 us; the launch traced here: 95.5 us
  waiting for transfers between devices  44 us (46%)
  starting transfers between devices  30.8 us (32%)
  Pallas kernels  17.7 us (18%)
  between operations  1.05 us (1%)
  local copies, waits for them, and re-layouts  0.99 us (1%)
    ppermute x24, waiting for transfers between devices, swap(): return lax.ppermute(value, AXES, [(i, i ^ mask) for i in range(total)])  44 us
    ppermute x24, starting transfers between devices, swap(): return lax.ppermute(value, AXES, [(i, i ^ mask) for i in range(total)])  30.8 us
    pallas_call x14, Pallas kernels, stage(): pl.pallas_call(kernel, out_shape=[shape(*out) for out in outs], in_specs=...  17.7 us
  transfers between devices with their start and end apart: 24, of which 18 were waited for; matrix products, arithmetic and copies ran while one was open for 1% of the time, Pallas kernels for 4%

profile of v2, /device:TPU:0, one launch (start us, length us, event | category | flops | bytes accessed | tf_op | source)
XLA Modules:
  0.0 95.5 jit_solution(9688395366656041294)
XLA Ops:
  0.6 5.6 %shard_map.140 = (f32[16,3584]{1,0:T(8,128)S(1)}, bf16[16,3584]{1,0:T(8,128)(2,1)S(1)}, f32[16,3584]{1,0:T(8,128)S(1)}) custom-call(bf16[32,1792]{1,0:T(8,128)(2,1)} %x_hbm.1, bf16[1792,3584]{1,0:T(8,128)(2,1)} %w_hbm.1, bf16[32,3584]{1,0:T(8,128)(2,1)} %resid_hbm.1), custom_call_target="tpu_custom_call" | custom-call | flops 5911042048 | bytes 27845056 | tf_op jit(solution)/shard_map/pallas_call | solution.py:29
  6.2 3.0 %collective-permute-start = (bf16[16,3584]{1,0:T(8,128)(2,1)S(1)}, bf16[16,3584]{1,0:T(8,128)(2,1)S(1)}, u32[]{:S(2)}, u32[]{:S(2)}) collective-permute-start(bf16[16,3584]{1,0:T(8,128)(2,1)S(1)} %get-tuple-element.29), channel_id=1, source_target_pairs={{0,1},{1,0},{2,3},{3,2},{4,5},{5,4},{6,7},{7,6},{8,9},{9,8},{10,11... | collective-permute-start | bytes 344072 | tf_op jit(solution)/shard_map/ppermute | solution.py:46
  9.3 3.1 %collective-permute-done.refs_0_ = bf16[16,3584]{1,0:T(8,128)(2,1)S(1)} collective-permute-done((bf16[16,3584]{1,0:T(8,128)(2,1)S(1)}, bf16[16,3584]{1,0:T(8,128)(2,1)S(1)}, u32[]{:S(2)}, u32[]{:S(2)}) %collective-permute-start) | collective-permute-done | bytes 114720 | tf_op jit(solution)/shard_map/ppermute | solution.py:46
  12.5 3.9 %collective-permute-start.1 = (bf16[16,3584]{1,0:T(8,128)(2,1)S(1)}, bf16[16,3584]{1,0:T(8,128)(2,1)S(1)}, u32[]{:S(2)}, u32[]{:S(2)}) collective-permute-start(bf16[16,3584]{1,0:T(8,128)(2,1)S(1)} %get-tuple-element.32), channel_id=1, source_target_pairs={{0,6},{1,7},{2,4},{3,5},{4,2},{5,3},{6,0},{7,1},{8,14},{9,15},{10,... | collective-permute-start | bytes 344072 | tf_op jit(solution)/shard_map/ppermute | solution.py:46
  17.1 3.3 %collective-permute-done.1.refs_0_ = bf16[16,3584]{1,0:T(8,128)(2,1)S(1)} collective-permute-done((bf16[16,3584]{1,0:T(8,128)(2,1)S(1)}, bf16[16,3584]{1,0:T(8,128)(2,1)S(1)}, u32[]{:S(2)}, u32[]{:S(2)}) %collective-permute-start.1) | collective-permute-done | bytes 114720 | tf_op jit(solution)/shard_map/ppermute | solution.py:46
  20.3 4.9 %collective-permute-done.2.refs_1_ = bf16[16,3584]{1,0:T(8,128)(2,1)S(1)} collective-permute-done((bf16[16,3584]{1,0:T(8,128)(2,1)S(1)}, bf16[16,3584]{1,0:T(8,128)(2,1)S(1)}, u32[]{:S(2)}, u32[]{:S(2)}) %collective-permute-start.2) | collective-permute-done | bytes 114720 | tf_op jit(solution)/shard_map/ppermute | solution.py:46
  25.5 2.5 %collective-permute-start.4 = (bf16[16,3584]{1,0:T(8,128)(2,1)S(1)}, bf16[16,3584]{1,0:T(8,128)(2,1)S(1)}, u32[]{:S(2)}, u32[]{:S(2)}) collective-permute-start(bf16[16,3584]{1,0:T(8,128)(2,1)S(1)} %shard_map.142.refs_0_), channel_id=1, source_target_pairs={{0,17},{1,16},{2,19},{3,18},{4,21},{5,20},{6,23},{7,22},{8,25},{9,... | collective-permute-start | bytes 344072 | tf_op jit(solution)/shard_map/ppermute | solution.py:46
  29.0 3.0 %collective-permute-done.4.refs_1_ = bf16[16,3584]{1,0:T(8,128)(2,1)S(1)} collective-permute-done((bf16[16,3584]{1,0:T(8,128)(2,1)S(1)}, bf16[16,3584]{1,0:T(8,128)(2,1)S(1)}, u32[]{:S(2)}, u32[]{:S(2)}) %collective-permute-start.4) | collective-permute-done | bytes 114720 | tf_op jit(solution)/shard_map/ppermute | solution.py:46
  32.0 1.2 %collective-permute-done.5.refs_2_ = bf16[16,3584]{1,0:T(8,128)(2,1)S(1)} collective-permute-done((bf16[16,3584]{1,0:T(8,128)(2,1)S(1)}, bf16[16,3584]{1,0:T(8,128)(2,1)S(1)}, u32[]{:S(2)}, u32[]{:S(2)}) %collective-permute-start.5) | collective-permute-done | bytes 114720 | tf_op jit(solution)/shard_map/ppermute | solution.py:46
  33.6 1.8 %collective-permute-done.7.theirs_ref = bf16[2,2,16,3584]{3,2,1,0:T(8,128)(2,1)S(1)} collective-permute-done((bf16[2,2,16,3584]{3,2,1,0:T(8,128)(2,1)S(1)}, bf16[2,2,16,3584]{3,2,1,0:T(8,128)(2,1)S(1)}, u32[]{:S(2)}, u32[]{:S(2)}) %collective-permute-start.7) | collective-permute-done | bytes 458784 | tf_op jit(solution)/shard_map/ppermute | solution.py:46
  35.4 3.4 %shard_map.144 = (bf16[128,2048]{1,0:T(8,128)(2,1)}, bf16[128,2048]{1,0:T(8,128)(2,1)S(1)}, f32[2,32,1792]{2,1,0:T(8,128)S(1)}, bf16[2,32,1792]{2,1,0:T(8,128)(2,1)S(1)}) custom-call(bf16[2,2,16,3584]{3,2,1,0:T(8,128)(2,1)S(1)} %shard_map.143.mine_ref.clean_ref, bf16[2,2,16,3584]{3,2,1,0:T(8,128)(2,1)S(1)} %collective-permute-done.7.theirs_ref, ...), custom_call_target="tpu_custom_call" | custom-call | flops 5018572288 | bytes 28020096 | tf_op jit(solution)/shard_map/pallas_call | solution.py:29
  39.0 1.1 %shard_map.145 = (f32[2,32,1792]{2,1,0:T(8,128)S(1)}, bf16[2,32,1792]{2,1,0:T(8,128)(2,1)S(1)}) custom-call(bf16[128,2048]{1,0:T(8,128)(2,1)S(1)} %get-tuple-element.34.hold_ref, bf16[2048,3584]{1,0:T(8,128)(2,1)S(1)} %bitcast.10), custom_call_target="tpu_custom_call" | custom-call | flops 3139524096 | bytes 13340032 | tf_op jit(solution)/shard_map/pallas_call | solution.py:29
  40.7 2.1 %collective-permute-start.10 = (bf16[32,1792]{1,0:T(8,128)(2,1)S(1)}, bf16[32,1792]{1,0:T(8,128)(2,1)S(1)}, u32[]{:S(2)}, u32[]{:S(2)}) collective-permute-start(bf16[32,1792]{1,0:T(8,128)(2,1)S(1)} %get-tuple-element.40), channel_id=1, source_target_pairs={{0,17},{1,16},{2,19},{3,18},{4,21},{5,20},{6,23},{7,22},{8,25},{9,... | collective-permute-start | bytes 344072 | tf_op jit(solution)/shard_map/ppermute | solution.py:46
  44.4 3.3 %collective-permute-done.10.refs_0_ = bf16[32,1792]{1,0:T(8,128)(2,1)S(1)} collective-permute-done((bf16[32,1792]{1,0:T(8,128)(2,1)S(1)}, bf16[32,1792]{1,0:T(8,128)(2,1)S(1)}, u32[]{:S(2)}, u32[]{:S(2)}) %collective-permute-start.10) | collective-permute-done | bytes 114720 | tf_op jit(solution)/shard_map/ppermute | solution.py:46
  47.6 1.4 %collective-permute-done.11.refs_1_ = bf16[32,1792]{1,0:T(8,128)(2,1)S(1)} collective-permute-done((bf16[32,1792]{1,0:T(8,128)(2,1)S(1)}, bf16[32,1792]{1,0:T(8,128)(2,1)S(1)}, u32[]{:S(2)}, u32[]{:S(2)}) %collective-permute-start.11) | collective-permute-done | bytes 114720 | tf_op jit(solution)/shard_map/ppermute | solution.py:46
  49.6 2.9 %collective-permute-start.14 = (bf16[32,1792]{1,0:T(8,128)(2,1)S(1)}, bf16[32,1792]{1,0:T(8,128)(2,1)S(1)}, u32[]{:S(2)}, u32[]{:S(2)}) collective-permute-start(bf16[32,1792]{1,0:T(8,128)(2,1)S(1)} %get-tuple-element.44), channel_id=1, source_target_pairs={{0,4},{1,5},{2,6},{3,7},{4,0},{5,1},{6,2},{7,3},{8,12},{9,13},{10,... | collective-permute-start | bytes 344072 | tf_op jit(solution)/shard_map/ppermute | solution.py:46
  52.4 1.4 %collective-permute-start.15 = (bf16[32,1792]{1,0:T(8,128)(2,1)S(1)}, bf16[32,1792]{1,0:T(8,128)(2,1)S(1)}, u32[]{:S(2)}, u32[]{:S(2)}) collective-permute-start(bf16[32,1792]{1,0:T(8,128)(2,1)S(1)} %get-tuple-element.44), channel_id=1, source_target_pairs={{0,6},{1,7},{2,4},{3,5},{4,2},{5,3},{6,0},{7,1},{8,14},{9,15},{10,... | collective-permute-start | bytes 344072 | tf_op jit(solution)/shard_map/ppermute | solution.py:46
  53.9 1.9 %collective-permute-done.13.refs_0_ = bf16[32,1792]{1,0:T(8,128)(2,1)S(1)} collective-permute-done((bf16[32,1792]{1,0:T(8,128)(2,1)S(1)}, bf16[32,1792]{1,0:T(8,128)(2,1)S(1)}, u32[]{:S(2)}, u32[]{:S(2)}) %collective-permute-start.13) | collective-permute-done | bytes 114720 | tf_op jit(solution)/shard_map/ppermute | solution.py:46
  55.8 5.6 %collective-permute-done.14.refs_1_ = bf16[32,1792]{1,0:T(8,128)(2,1)S(1)} collective-permute-done((bf16[32,1792]{1,0:T(8,128)(2,1)S(1)}, bf16[32,1792]{1,0:T(8,128)(2,1)S(1)}, u32[]{:S(2)}, u32[]{:S(2)}) %collective-permute-start.14) | collective-permute-done | bytes 114720 | tf_op jit(solution)/shard_map/ppermute | solution.py:46
  61.5 1.5 %collective-permute-start.16 = (bf16[32,1792]{1,0:T(8,128)(2,1)S(1)}, bf16[32,1792]{1,0:T(8,128)(2,1)S(1)}, u32[]{:S(2)}, u32[]{:S(2)}) collective-permute-start(bf16[32,1792]{1,0:T(8,128)(2,1)S(1)} %shard_map.149.recon_ref), channel_id=1, source_target_pairs={{0,1},{1,0},{2,3},{3,2},{4,5},{5,4},{6,7},{7,6},{8,9},{9,8},{10,11... | collective-permute-start | bytes 344072 | tf_op jit(solution)/shard_map/ppermute | solution.py:46
  63.1 2.4 %shard_map.150 = (f32[64,1792]{1,0:T(8,128)S(1)}, f32[64,1792]{1,0:T(8,128)S(1)}) custom-call(bf16[2,2,16,3584]{3,2,1,0:T(8,128)(2,1)S(1)} %shard_map.143.mine_ref.clean_ref, bf16[32,1792]{1,0:T(8,128)(2,1)S(1)} %shard_map.149.recon_ref, f32[1,3584]{1,0:T(1,128)S(1)} %reshape.53.gain_ref, bf16[3584,1792]{1,0:T(8,128)(2,1)S(1)} %bitcast.12, ...), custom_call_target="tpu_custom_call" | custom-call | flops 822083584 | bytes 12845056 | tf_op jit(solution)/shard_map/pallas_call | solution.py:29
  66.3 2.9 %shard_map.151 = (f32[64,3584]{1,0:T(8,128)S(1)}, bf16[64,1792]{1,0:T(8,128)(2,1)S(1)}, bf16[64,896]{1,0:T(8,128)(2,1)S(1)}) custom-call(bf16[2,2,16,3584]{3,2,1,0:T(8,128)(2,1)S(1)} %shard_map.143.mine_ref.clean_ref, bf16[32,1792]{1,0:T(8,128)(2,1)S(1)} %shard_map.149.recon_ref, bf16[32,1792]{1,0:T(8,128)(2,1)S(1)} %collective-permute-done.16.got_ref, ...), custom_call_target="tpu_custom_call" | custom-call | flops 1233125376 | bytes 19267584 | tf_op jit(solution)/shard_map/pallas_call | solution.py:29
  69.3 1.7 %shard_map.152 = (bf16[64,896]{1,0:T(8,128)(2,1)S(1)}, bf16[64,896]{1,0:T(8,128)(2,1)S(1)}, f32[64,896]{1,0:T(8,128)S(1)}) custom-call(bf16[64,1792]{1,0:T(8,128)(2,1)S(1)} %get-tuple-element.49.act_ref, bf16[1792,3584]{1,0:T(8,128)(2,1)S(1)} %bitcast.8), custom_call_target="tpu_custom_call" | custom-call | flops 411041792 | bytes 6422528 | tf_op jit(solution)/shard_map/pallas_call | solution.py:29
  71.0 2.4 %collective-permute-start.17 = (bf16[64,896]{1,0:T(8,128)(2,1)S(1)}, bf16[64,896]{1,0:T(8,128)(2,1)S(1)}, u32[]{:S(2)}, u32[]{:S(2)}) collective-permute-start(bf16[64,896]{1,0:T(8,128)(2,1)S(1)} %get-tuple-element.51), channel_id=1, source_target_pairs={{0,6},{1,7},{2,4},{3,5},{4,2},{5,3},{6,0},{7,1},{8,14},{9,15},{10,... | collective-permute-start | bytes 344072 | tf_op jit(solution)/shard_map/ppermute | solution.py:46
  74.3 1.1 %collective-permute-start.19 = (bf16[64,896]{1,0:T(8,128)(2,1)S(1)}, bf16[64,896]{1,0:T(8,128)(2,1)S(1)}, u32[]{:S(2)}, u32[]{:S(2)}) collective-permute-start(bf16[64,896]{1,0:T(8,128)(2,1)S(1)} %get-tuple-element.53), channel_id=1, source_target_pairs={{0,2},{1,3},{2,0},{3,1},{4,6},{5,7},{6,4},{7,5},{8,10},{9,11},{10,... | collective-permute-start | bytes 344072 | tf_op jit(solution)/shard_map/ppermute | solution.py:46
  75.4 3.3 %collective-permute-done.17.refs_0_ = bf16[64,896]{1,0:T(8,128)(2,1)S(1)} collective-permute-done((bf16[64,896]{1,0:T(8,128)(2,1)S(1)}, bf16[64,896]{1,0:T(8,128)(2,1)S(1)}, u32[]{:S(2)}, u32[]{:S(2)}) %collective-permute-start.17) | collective-permute-done | bytes 114720 | tf_op jit(solution)/shard_map/ppermute | solution.py:46
  78.7 3.6 %collective-permute-done.18.refs_1_ = bf16[64,896]{1,0:T(8,128)(2,1)S(1)} collective-permute-done((bf16[64,896]{1,0:T(8,128)(2,1)S(1)}, bf16[64,896]{1,0:T(8,128)(2,1)S(1)}, u32[]{:S(2)}, u32[]{:S(2)}) %collective-permute-start.18) | collective-permute-done | bytes 114720 | tf_op jit(solution)/shard_map/ppermute | solution.py:46
  82.4 1.5 %collective-permute-start.20 = (bf16[64,896]{1,0:T(8,128)(2,1)S(1)}, bf16[64,896]{1,0:T(8,128)(2,1)S(1)}, u32[]{:S(2)}, u32[]{:S(2)}) collective-permute-start(bf16[64,896]{1,0:T(8,128)(2,1)S(1)} %shard_map.153), channel_id=1, source_target_pairs={{0,1},{1,0},{2,3},{3,2},{4,5},{5,4},{6,7},{7,6},{8,9},{9,8},{10,11... | collective-permute-start | bytes 344072 | tf_op jit(solution)/shard_map/ppermute | solution.py:46
  83.8 3.4 %collective-permute-done.20 = bf16[64,896]{1,0:T(8,128)(2,1)S(1)} collective-permute-done((bf16[64,896]{1,0:T(8,128)(2,1)S(1)}, bf16[64,896]{1,0:T(8,128)(2,1)S(1)}, u32[]{:S(2)}, u32[]{:S(2)}) %collective-permute-start.20) | collective-permute-done | bytes 114720 | tf_op jit(solution)/shard_map/ppermute | solution.py:46
  87.4 2.7 %collective-permute-start.22 = (f32[1,64]{1,0:T(1,128)S(1)}, f32[1,64]{1,0:T(1,128)S(1)}, u32[]{:S(2)}, u32[]{:S(2)}) collective-permute-start(f32[1,64]{1,0:T(1,128)S(1)} %bitcast.19), channel_id=1, source_target_pairs={{0,6},{1,7},{2,4},{3,5},{4,2},{5,3},{6,0},{7,1},{8,14},{9,15},{10,... | collective-permute-start | bytes 776 | tf_op jit(solution)/shard_map/ppermute | solution.py:46
  91.7 1.2 %collective-permute-done.22 = f32[1,64]{1,0:T(1,128)S(1)} collective-permute-done((f32[1,64]{1,0:T(1,128)S(1)}, f32[1,64]{1,0:T(1,128)S(1)}, u32[]{:S(2)}, u32[]{:S(2)}) %collective-permute-start.22) | collective-permute-done | bytes 288 | tf_op jit(solution)/shard_map/ppermute | solution.py:46
  92.9 1.7 %collective-permute-done.21 = f32[1,64]{1,0:T(1,128)S(1)} collective-permute-done((f32[1,64]{1,0:T(1,128)S(1)}, f32[1,64]{1,0:T(1,128)S(1)}, u32[]{:S(2)}, u32[]{:S(2)}) %collective-permute-start.21) | collective-permute-done | bytes 288 | tf_op jit(solution)/shard_map/ppermute | solution.py:46
  (91 shorter events, 9.7 us)
Async XLA Ops:
  6.2 6.2 %collective-permute-start = (bf16[16,3584]{1,0:T(8,128)(2,1)S(1)}, bf16[16,3584]{1,0:T(8,128)(2,1)S(1)}, u32[]{:S(2)}, u32[]{:S(2)}) collective-permute-start(bf16[16,3584]{1,0:T(8,128)(2,1)S(1)} %get-tuple-element.29), channel_id=1, source_target_pairs={{0,1},{1,0},{2,3},{3,2},{4,5},{5,4},{6,7},{7,6},{8,9},{9,8},{10,11... | collective-permute-start | bytes 344072 | tf_op jit(solution)/shard_map/ppermute | solution.py:46
  12.4 22.9 %slice-start.16 = ((s8[14680064]{0:T(1024)(128)(4,1)}), s8[4194304]{0:T(1024)(128)(4,1)S(1)}, s32[]{:S(2)}) async-start(s8[14680064]{0:T(1024)(128)(4,1)} %bitcast.15), calls=%async_computation.16 | async-start | bytes 8388608
  12.4 22.9 %slice-start.17 = ((s8[14680064]{0:T(1024)(128)(4,1)}), s8[4194304]{0:T(1024)(128)(4,1)S(1)}, s32[]{:S(2)}) async-start(s8[14680064]{0:T(1024)(128)(4,1)} %bitcast.15), calls=%async_computation.17 | async-start | bytes 8388608
  12.4 22.9 %slice-start.18 = ((s8[14680064]{0:T(1024)(128)(4,1)}), s8[4194304]{0:T(1024)(128)(4,1)S(1)}, s32[]{:S(2)}) async-start(s8[14680064]{0:T(1024)(128)(4,1)} %bitcast.15), calls=%async_computation.18 | async-start | bytes 8388608
  12.5 7.8 %collective-permute-start.1 = (bf16[16,3584]{1,0:T(8,128)(2,1)S(1)}, bf16[16,3584]{1,0:T(8,128)(2,1)S(1)}, u32[]{:S(2)}, u32[]{:S(2)}) collective-permute-start(bf16[16,3584]{1,0:T(8,128)(2,1)S(1)} %get-tuple-element.32), channel_id=1, source_target_pairs={{0,6},{1,7},{2,4},{3,5},{4,2},{5,3},{6,0},{7,1},{8,14},{9,15},{10,... | collective-permute-start | bytes 344072 | tf_op jit(solution)/shard_map/ppermute | solution.py:46
  16.4 8.8 %collective-permute-start.2 = (bf16[16,3584]{1,0:T(8,128)(2,1)S(1)}, bf16[16,3584]{1,0:T(8,128)(2,1)S(1)}, u32[]{:S(2)}, u32[]{:S(2)}) collective-permute-start(bf16[16,3584]{1,0:T(8,128)(2,1)S(1)} %get-tuple-element.32), channel_id=1, source_target_pairs={{0,4},{1,5},{2,6},{3,7},{4,0},{5,1},{6,2},{7,3},{8,12},{9,13},{10,... | collective-permute-start | bytes 344072 | tf_op jit(solution)/shard_map/ppermute | solution.py:46
  16.4 8.8 %collective-permute-start.3 = (bf16[16,3584]{1,0:T(8,128)(2,1)S(1)}, bf16[16,3584]{1,0:T(8,128)(2,1)S(1)}, u32[]{:S(2)}, u32[]{:S(2)}) collective-permute-start(bf16[16,3584]{1,0:T(8,128)(2,1)S(1)} %get-tuple-element.32), channel_id=1, source_target_pairs={{0,2},{1,3},{2,0},{3,1},{4,6},{5,7},{6,4},{7,5},{8,10},{9,11},{10,... | collective-permute-start | bytes 344072 | tf_op jit(solution)/shard_map/ppermute | solution.py:46
  25.5 6.5 %collective-permute-start.4 = (bf16[16,3584]{1,0:T(8,128)(2,1)S(1)}, bf16[16,3584]{1,0:T(8,128)(2,1)S(1)}, u32[]{:S(2)}, u32[]{:S(2)}) collective-permute-start(bf16[16,3584]{1,0:T(8,128)(2,1)S(1)} %shard_map.142.refs_0_), channel_id=1, source_target_pairs={{0,17},{1,16},{2,19},{3,18},{4,21},{5,20},{6,23},{7,22},{8,25},{9,... | collective-permute-start | bytes 344072 | tf_op jit(solution)/shard_map/ppermute | solution.py:46
  28.0 5.2 %collective-permute-start.5 = (bf16[16,3584]{1,0:T(8,128)(2,1)S(1)}, bf16[16,3584]{1,0:T(8,128)(2,1)S(1)}, u32[]{:S(2)}, u32[]{:S(2)}) collective-permute-start(bf16[16,3584]{1,0:T(8,128)(2,1)S(1)} %shard_map.142.refs_0_), channel_id=1, source_target_pairs={{0,1},{1,0},{2,3},{3,2},{4,5},{5,4},{6,7},{7,6},{8,9},{9,8},{10,11... | collective-permute-start | bytes 344072 | tf_op jit(solution)/shard_map/ppermute | solution.py:46
  28.5 4.9 %collective-permute-start.6 = (bf16[16,3584]{1,0:T(8,128)(2,1)S(1)}, bf16[16,3584]{1,0:T(8,128)(2,1)S(1)}, u32[]{:S(2)}, u32[]{:S(2)}) collective-permute-start(bf16[16,3584]{1,0:T(8,128)(2,1)S(1)} %shard_map.142.refs_0_), channel_id=1, source_target_pairs={{0,16},{1,17},{2,18},{3,19},{4,20},{5,21},{6,22},{7,23},{8,24},{9,... | collective-permute-start | bytes 344072 | tf_op jit(solution)/shard_map/ppermute | solution.py:46
  33.5 1.9 %collective-permute-start.7 = (bf16[2,2,16,3584]{3,2,1,0:T(8,128)(2,1)S(1)}, bf16[2,2,16,3584]{3,2,1,0:T(8,128)(2,1)S(1)}, u32[]{:S(2)}, u32[]{:S(2)}) collective-permute-start(bf16[2,2,16,3584]{3,2,1,0:T(8,128)(2,1)S(1)} %shard_map.143.mine_ref.clean_ref), channel_id=1, source_target_pairs={{0,8},{1,9},{2,10},{3,11},{4,12},{5,13},{6,14},{7,15},{8,0},{9,1},... | collective-permute-start | bytes 1376264 | tf_op jit(solution)/shard_map/ppermute | solution.py:46
  38.8 1.8 %collective-permute-start.9 = (bf16[2,32,1792]{2,1,0:T(8,128)(2,1)S(1)}, bf16[2,32,1792]{2,1,0:T(8,128)(2,1)S(1)}, u32[]{:S(2)}, u32[]{:S(2)}) collective-permute-start(bf16[2,32,1792]{2,1,0:T(8,128)(2,1)S(1)} %get-tuple-element.39), channel_id=1, source_target_pairs={{0,8},{1,9},{2,10},{3,11},{4,12},{5,13},{6,14},{7,15},{8,0},{9,1},... | collective-permute-start | bytes 688136 | tf_op jit(solution)/shard_map/ppermute | solution.py:46
  40.1 3.3 %collective-permute-start.8 = (bf16[2,32,1792]{2,1,0:T(8,128)(2,1)S(1)}, bf16[2,32,1792]{2,1,0:T(8,128)(2,1)S(1)}, u32[]{:S(2)}, u32[]{:S(2)}) collective-permute-start(bf16[2,32,1792]{2,1,0:T(8,128)(2,1)S(1)} %get-tuple-element.36), channel_id=1, source_target_pairs={{0,8},{1,9},{2,10},{3,11},{4,12},{5,13},{6,14},{7,15},{8,0},{9,1},... | collective-permute-start | bytes 688136 | tf_op jit(solution)/shard_map/ppermute | solution.py:46
  40.7 7.0 %collective-permute-start.10 = (bf16[32,1792]{1,0:T(8,128)(2,1)S(1)}, bf16[32,1792]{1,0:T(8,128)(2,1)S(1)}, u32[]{:S(2)}, u32[]{:S(2)}) collective-permute-start(bf16[32,1792]{1,0:T(8,128)(2,1)S(1)} %get-tuple-element.40), channel_id=1, source_target_pairs={{0,17},{1,16},{2,19},{3,18},{4,21},{5,20},{6,23},{7,22},{8,25},{9,... | collective-permute-start | bytes 344072 | tf_op jit(solution)/shard_map/ppermute | solution.py:46
  42.8 6.2 %collective-permute-start.11 = (bf16[32,1792]{1,0:T(8,128)(2,1)S(1)}, bf16[32,1792]{1,0:T(8,128)(2,1)S(1)}, u32[]{:S(2)}, u32[]{:S(2)}) collective-permute-start(bf16[32,1792]{1,0:T(8,128)(2,1)S(1)} %get-tuple-element.41), channel_id=1, source_target_pairs={{0,1},{1,0},{2,3},{3,2},{4,5},{5,4},{6,7},{7,6},{8,9},{9,8},{10,11... | collective-permute-start | bytes 344072 | tf_op jit(solution)/shard_map/ppermute | solution.py:46
  43.5 5.8 %collective-permute-start.12 = (bf16[32,1792]{1,0:T(8,128)(2,1)S(1)}, bf16[32,1792]{1,0:T(8,128)(2,1)S(1)}, u32[]{:S(2)}, u32[]{:S(2)}) collective-permute-start(bf16[32,1792]{1,0:T(8,128)(2,1)S(1)} %get-tuple-element.42), channel_id=1, source_target_pairs={{0,16},{1,17},{2,18},{3,19},{4,20},{5,21},{6,22},{7,23},{8,24},{9,... | collective-permute-start | bytes 344072 | tf_op jit(solution)/shard_map/ppermute | solution.py:46
  49.3 13.7 %slice-start.8 = ((s8[12845056]{0:T(1024)(128)(4,1)}), s8[4194304]{0:T(1024)(128)(4,1)S(1)}, s32[]{:S(2)}) async-start(s8[12845056]{0:T(1024)(128)(4,1)} %bitcast.11), calls=%async_computation.8 | async-start | bytes 8388608
  49.3 13.7 %slice-start.9 = ((s8[12845056]{0:T(1024)(128)(4,1)}), s8[4194304]{0:T(1024)(128)(4,1)S(1)}, s32[]{:S(2)}) async-start(s8[12845056]{0:T(1024)(128)(4,1)} %bitcast.11), calls=%async_computation.9 | async-start | bytes 8388608
  49.3 13.7 %slice-start.10 = ((s8[12845056]{0:T(1024)(128)(4,1)}), s8[4194304]{0:T(1024)(128)(4,1)S(1)}, s32[]{:S(2)}) async-start(s8[12845056]{0:T(1024)(128)(4,1)} %bitcast.11), calls=%async_computation.10 | async-start | bytes 8388608
  49.3 13.7 %slice-start.12 = ((s8[12845056]{0:T(1024)(128)(4,1)}), s8[4194304]{0:T(1024)(128)(4,1)S(1)}, s32[]{:S(2)}) async-start(s8[12845056]{0:T(1024)(128)(4,1)} %bitcast.13), calls=%async_computation.12 | async-start | bytes 8388608
  49.3 13.7 %slice-start.13 = ((s8[12845056]{0:T(1024)(128)(4,1)}), s8[4194304]{0:T(1024)(128)(4,1)S(1)}, s32[]{:S(2)}) async-start(s8[12845056]{0:T(1024)(128)(4,1)} %bitcast.13), calls=%async_computation.13 | async-start | bytes 8388608
  49.4 6.4 %collective-permute-start.13 = (bf16[32,1792]{1,0:T(8,128)(2,1)S(1)}, bf16[32,1792]{1,0:T(8,128)(2,1)S(1)}, u32[]{:S(2)}, u32[]{:S(2)}) collective-permute-start(bf16[32,1792]{1,0:T(8,128)(2,1)S(1)} %get-tuple-element.44), channel_id=1, source_target_pairs={{0,2},{1,3},{2,0},{3,1},{4,6},{5,7},{6,4},{7,5},{8,10},{9,11},{10,... | collective-permute-start | bytes 344072 | tf_op jit(solution)/shard_map/ppermute | solution.py:46
  49.6 11.8 %collective-permute-start.14 = (bf16[32,1792]{1,0:T(8,128)(2,1)S(1)}, bf16[32,1792]{1,0:T(8,128)(2,1)S(1)}, u32[]{:S(2)}, u32[]{:S(2)}) collective-permute-start(bf16[32,1792]{1,0:T(8,128)(2,1)S(1)} %get-tuple-element.44), channel_id=1, source_target_pairs={{0,4},{1,5},{2,6},{3,7},{4,0},{5,1},{6,2},{7,3},{8,12},{9,13},{10,... | collective-permute-start | bytes 344072 | tf_op jit(solution)/shard_map/ppermute | solution.py:46
  52.4 9.0 %collective-permute-start.15 = (bf16[32,1792]{1,0:T(8,128)(2,1)S(1)}, bf16[32,1792]{1,0:T(8,128)(2,1)S(1)}, u32[]{:S(2)}, u32[]{:S(2)}) collective-permute-start(bf16[32,1792]{1,0:T(8,128)(2,1)S(1)} %get-tuple-element.44), channel_id=1, source_target_pairs={{0,6},{1,7},{2,4},{3,5},{4,2},{5,3},{6,0},{7,1},{8,14},{9,15},{10,... | collective-permute-start | bytes 344072 | tf_op jit(solution)/shard_map/ppermute | solution.py:46
  61.5 4.9 %collective-permute-start.16 = (bf16[32,1792]{1,0:T(8,128)(2,1)S(1)}, bf16[32,1792]{1,0:T(8,128)(2,1)S(1)}, u32[]{:S(2)}, u32[]{:S(2)}) collective-permute-start(bf16[32,1792]{1,0:T(8,128)(2,1)S(1)} %shard_map.149.recon_ref), channel_id=1, source_target_pairs={{0,1},{1,0},{2,3},{3,2},{4,5},{5,4},{6,7},{7,6},{8,9},{9,8},{10,11... | collective-permute-start | bytes 344072 | tf_op jit(solution)/shard_map/ppermute | solution.py:46
  71.0 7.7 %collective-permute-start.17 = (bf16[64,896]{1,0:T(8,128)(2,1)S(1)}, bf16[64,896]{1,0:T(8,128)(2,1)S(1)}, u32[]{:S(2)}, u32[]{:S(2)}) collective-permute-start(bf16[64,896]{1,0:T(8,128)(2,1)S(1)} %get-tuple-element.51), channel_id=1, source_target_pairs={{0,6},{1,7},{2,4},{3,5},{4,2},{5,3},{6,0},{7,1},{8,14},{9,15},{10,... | collective-permute-start | bytes 344072 | tf_op jit(solution)/shard_map/ppermute | solution.py:46
  73.4 8.9 %collective-permute-start.18 = (bf16[64,896]{1,0:T(8,128)(2,1)S(1)}, bf16[64,896]{1,0:T(8,128)(2,1)S(1)}, u32[]{:S(2)}, u32[]{:S(2)}) collective-permute-start(bf16[64,896]{1,0:T(8,128)(2,1)S(1)} %get-tuple-element.52), channel_id=1, source_target_pairs={{0,4},{1,5},{2,6},{3,7},{4,0},{5,1},{6,2},{7,3},{8,12},{9,13},{10,... | collective-permute-start | bytes 344072 | tf_op jit(solution)/shard_map/ppermute | solution.py:46
  74.3 8.0 %collective-permute-start.19 = (bf16[64,896]{1,0:T(8,128)(2,1)S(1)}, bf16[64,896]{1,0:T(8,128)(2,1)S(1)}, u32[]{:S(2)}, u32[]{:S(2)}) collective-permute-start(bf16[64,896]{1,0:T(8,128)(2,1)S(1)} %get-tuple-element.53), channel_id=1, source_target_pairs={{0,2},{1,3},{2,0},{3,1},{4,6},{5,7},{6,4},{7,5},{8,10},{9,11},{10,... | collective-permute-start | bytes 344072 | tf_op jit(solution)/shard_map/ppermute | solution.py:46
  82.4 4.9 %collective-permute-start.20 = (bf16[64,896]{1,0:T(8,128)(2,1)S(1)}, bf16[64,896]{1,0:T(8,128)(2,1)S(1)}, u32[]{:S(2)}, u32[]{:S(2)}) collective-permute-start(bf16[64,896]{1,0:T(8,128)(2,1)S(1)} %shard_map.153), channel_id=1, source_target_pairs={{0,1},{1,0},{2,3},{3,2},{4,5},{5,4},{6,7},{7,6},{8,9},{9,8},{10,11... | collective-permute-start | bytes 344072 | tf_op jit(solution)/shard_map/ppermute | solution.py:46
  87.4 4.3 %collective-permute-start.23 = (f32[1,64]{1,0:T(1,128)S(1)}, f32[1,64]{1,0:T(1,128)S(1)}, u32[]{:S(2)}, u32[]{:S(2)}) collective-permute-start(f32[1,64]{1,0:T(1,128)S(1)} %bitcast.18), channel_id=1, source_target_pairs={{0,2},{1,3},{2,0},{3,1},{4,6},{5,7},{6,4},{7,5},{8,10},{9,11},{10,... | collective-permute-start | bytes 776 | tf_op jit(solution)/shard_map/ppermute | solution.py:46
  87.4 5.4 %collective-permute-start.22 = (f32[1,64]{1,0:T(1,128)S(1)}, f32[1,64]{1,0:T(1,128)S(1)}, u32[]{:S(2)}, u32[]{:S(2)}) collective-permute-start(f32[1,64]{1,0:T(1,128)S(1)} %bitcast.19), channel_id=1, source_target_pairs={{0,6},{1,7},{2,4},{3,5},{4,2},{5,3},{6,0},{7,1},{8,14},{9,15},{10,... | collective-permute-start | bytes 776 | tf_op jit(solution)/shard_map/ppermute | solution.py:46
  90.1 4.5 %collective-permute-start.21 = (f32[1,64]{1,0:T(1,128)S(1)}, f32[1,64]{1,0:T(1,128)S(1)}, u32[]{:S(2)}, u32[]{:S(2)}) collective-permute-start(f32[1,64]{1,0:T(1,128)S(1)} %bitcast.20), channel_id=1, source_target_pairs={{0,4},{1,5},{2,6},{3,7},{4,0},{5,1},{6,2},{7,3},{8,12},{9,13},{10,... | collective-permute-start | bytes 776 | tf_op jit(solution)/shard_map/ppermute | solution.py:46
  (16 other events, 147.2 us)
